TPU v7x, 128 devices: a whole 4x4x4 slice. The times are simulated.
128 devices in a mesh: blk: 16 (over y_hi, x, core), tp: 8 (over z, y_lo).
Axes of the slice: x: 4, y: 4 (y_hi: 2, y_lo: 2; y = y_hi * 2 + y_lo), z: 4, core: 2. Of those that a mesh axis runs over, the one named last changes fastest.
Arguments:
- text_emb: bfloat16 [49152, 1024], P('blk', 'tp'), may hold values from -4 to 4
- image_emb: bfloat16 [49152, 1024], P(('blk', 'tp')), may hold values from -4 to 4
- logit_scale: float32 [1], replicated, may hold values from 4 to 12
- logit_bias: float32 [1], replicated, may hold values from -3 to -1
- bucket: int32 [49152], replicated, may hold values from 0 to 3
- positive: int32 [49152], replicated, may hold values from 0 to 49151, as said below
- blocks: int32 [384, 16, 3], replicated, may hold values from -1 to 2, as said below
Outputs:
- text_grad: bfloat16 [49152, 1024], P('blk', 'tp')
- image_grad: bfloat16 [49152, 1024], P(('blk', 'tp'))
Inputs may be any that keep to these rules, and one draw needn't show every extreme that they name: positive[i] lies in the same 128-row tile as i, and within each tile the entries are a permutation of that tile's rows. `blocks`: each entry is a tile of the named shard or -1 for an unused slot; slot 0 is never -1; the used slots of one text tile and shard name different tiles; for the text tile's own blk index, slot 0 names the text tile's own tile.
All inputs are finite; a program needn't handle non-finite values.
Results may differ from a plain program's by a relative error of at most 0.015.
Values may be sent and summed in bfloat16 or wider, within the bound.
A program may use at most 128 MiB of HBM per device.

v0:
```python
import jax
import jax.numpy as jnp
from jax import lax
from jax.sharding import PartitionSpec as P

TILE = 128
SLOTS = 3


def unit_rows(raw_rows):
    values = raw_rows.astype(jnp.float32)
    scales = lax.rsqrt(jnp.sum(values * values, axis=-1, keepdims=True) + 1e-06)
    return (values * scales, scales)


def grad_rows(raw_rows, scales, upstream):
    unit_float = raw_rows.astype(jnp.float32) * scales
    return (
        scales * (upstream - unit_float * jnp.sum(unit_float * upstream, axis=-1, keepdims=True))
    ).astype(jnp.bfloat16)


def pair_weights(
    text_part, text_ids, image_part, image_ids, live_mask, scale_value, bias_value, positive, bucket
):
    tile_rows = text_part.shape[1]
    products = jnp.einsum("cid,cjd->cij", text_part, image_part, preferred_element_type=jnp.float32)
    logits = scale_value * products + bias_value
    columns = image_ids[:, None] * tile_rows + jnp.arange(tile_rows, dtype=jnp.int32)[None, :]
    row_positive = positive.reshape(-1, tile_rows)[text_ids]
    row_bucket = bucket.reshape(-1, tile_rows)[text_ids]
    col_bucket = bucket.reshape(-1, tile_rows)[image_ids]
    matched = row_positive[:, :, None] == columns[:, None, :]
    labels = jnp.where(matched, 1.0, -1.0).astype(jnp.float32)
    kept_pairs = jnp.logical_or(matched, row_bucket[:, :, None] == col_bucket[:, None, :])
    pair_mask = (
        jnp.where(kept_pairs, 1.0, 0.0).astype(jnp.float32)
        * jnp.where(live_mask, 1.0, 0.0).astype(jnp.float32)[:, None, None]
    )
    return (scale_value * pair_mask * -labels * jax.nn.sigmoid(-labels * logits)).astype(
        jnp.bfloat16
    )


def per_device(text_emb, image_emb, logit_scale, logit_bias, bucket, positive, blocks):
    text_local = lax.all_to_all(text_emb, "tp", split_axis=0, concat_axis=1, tiled=True)
    text_float, text_scales = unit_rows(text_local)
    image_float, image_scales = unit_rows(image_emb)
    text_unit = text_float.astype(jnp.bfloat16)
    image_unit = image_float.astype(jnp.bfloat16)
    row_count = text_unit.shape[0]
    width = text_unit.shape[1]
    tile_count = row_count // TILE
    groups = lax.axis_size("tp")
    blk_index = lax.axis_index("blk")
    tp_index = lax.axis_index("tp")
    device = blk_index * groups + tp_index
    scale_value = logit_scale[0]
    bias_value = logit_bias[0]
    tile_range = jnp.arange(tile_count, dtype=jnp.int32)
    local_ids = device * tile_count + tile_range
    text_tiles = text_unit.reshape(tile_count, TILE, width)
    image_tiles = image_unit.reshape(tile_count, TILE, width)
    text_repeat = jnp.repeat(text_tiles, SLOTS, axis=0)
    text_ids = jnp.repeat(local_ids, SLOTS)
    own_blocks = lax.dynamic_slice_in_dim(blocks, device * tile_count, tile_count, 0)

    def listed_pairs(source, shard):
        listed = lax.dynamic_index_in_dim(own_blocks, source, 1, keepdims=False).reshape(-1)
        live_mask = listed >= 0
        local_tile = jnp.maximum(listed, 0)
        remote = shard.reshape(tile_count, TILE, width)[local_tile]
        remote_ids = (source * groups + tp_index) * tile_count + local_tile
        weights = pair_weights(
            text_repeat,
            text_ids,
            remote,
            remote_ids,
            live_mask,
            scale_value,
            bias_value,
            positive,
            bucket,
        )
        return (weights, remote, local_tile)

    def text_step(source, shard, text_acc):
        weights, remote, local_tile = listed_pairs(source, shard)
        update = jnp.einsum("cij,cjd->cid", weights, remote, preferred_element_type=jnp.float32)
        return text_acc + update.reshape(tile_count, SLOTS, TILE, width).sum(axis=1)

    def image_step(source, shard, image_acc):
        sender = source * groups + tp_index
        sender_blocks = lax.dynamic_slice_in_dim(blocks, sender * tile_count, tile_count, 0)
        listed = lax.dynamic_index_in_dim(sender_blocks, blk_index, 1, keepdims=False).reshape(-1)
        live_mask = listed >= 0
        local_tile = jnp.maximum(listed, 0)
        sender_text = jnp.repeat(shard.reshape(tile_count, TILE, width), SLOTS, axis=0)
        sender_ids = jnp.repeat(sender * tile_count + tile_range, SLOTS)
        mine = image_tiles[local_tile]
        weights = pair_weights(
            sender_text,
            sender_ids,
            mine,
            device * tile_count + local_tile,
            live_mask,
            scale_value,
            bias_value,
            positive,
            bucket,
        )
        update = jnp.einsum(
            "cij,cid->cjd", weights, sender_text, preferred_element_type=jnp.float32
        )
        return image_acc.at[local_tile].add(update)

    def over_shards(step_fn, piece, accum):
        count = piece.shape[0] // row_count

        def one_shard(offset, carried):
            shard = lax.dynamic_slice_in_dim(piece, offset * row_count, row_count, 0)
            return step_fn(offset, shard, carried)

        return lax.fori_loop(0, count, one_shard, accum)

    empty = jnp.zeros((tile_count, TILE, width), jnp.float32)
    text_acc = over_shards(text_step, lax.all_gather(image_unit, "blk", axis=0, tiled=True), empty)
    image_acc = over_shards(image_step, lax.all_gather(text_unit, "blk", axis=0, tiled=True), empty)
    text_grad_local = grad_rows(text_local, text_scales, text_acc.reshape(row_count, width))
    text_grad = lax.all_to_all(text_grad_local, "tp", split_axis=1, concat_axis=0, tiled=True)
    image_grad = grad_rows(image_emb, image_scales, image_acc.reshape(row_count, width))
    return (text_grad, image_grad)


def solution(mesh):
    in_specs = (P("blk", "tp"), P(("blk", "tp"), None), P(), P(), P(), P(), P())
    out_specs = (P("blk", "tp"), P(("blk", "tp"), None))
    return jax.shard_map(
        per_device, mesh=mesh, in_specs=in_specs, out_specs=out_specs, check_vma=False
    )
```

profile of v0, /device:TPU:1, one launch (start us, length us, event | category | flops | bytes accessed | tf_op | source)
XLA Modules:
  0.0 917.2 jit_solution(3994052237907883723)
XLA Ops:
  10.8 6.9 all-to-all-start
  22.6 6.8 all-to-all-done
  37.8 69.1 %all-gather.3.cloned.1.call-done = bf16[6144,1024]{1,0:T(8,128)(2,1)} async-done(((bf16[384,1024]{1,0:T(8,128)(2,1)}), bf16[6144,1024]{1,0:T(8,128)(2,1)}) %all-gather.3.cloned.1.call-update) | async-done | bytes 12582928 | tf_op jit(solution)/shard_map/all_gather | solution.py:127
  106.9 337.7 %while.34 = (s32[]{:T(128)}, f32[3,128,1024]{2,1,0:T(8,128)}, f32[]{:T(128)}, s32[9,128]{1,0:T(8,128)S(1)}, s32[]{:T(128)}, /*index=5*/s32[3,16,3]{2,0,1:T(4,128...) while((s32[]{:T(128)}, f32[3,128,1024]{2,1,0:T(8,128)}, ...), condition=%wide.region_4.5_spmd.clone, body=%wide.region_2.4_spmd.clone.sunk | while | flops 608506112 | bytes 50346900 | solution.py:124
  116.4 6.9 fusion.97
  180.8 7.1 fusion.97
  454.1 11.6 %all-to-all-done.1 = bf16[384,8,128]{2,0,1:T(8,128)(2,1)S(1)} async-done(((bf16[384,8,128]{2,0,1:T(8,128)(2,1)}), bf16[384,8,128]{2,0,1:T(8,128)(2,1)S(1)}, u32[]{:S(2)}, u32[]{:S(2)}) %all-to-all-start.1) | async-done | bytes 786464 | tf_op jit(solution)/shard_map/all_to_all | solution.py:130
  467.1 438.8 %while.33 = (s32[]{:T(128)}, f32[3,128,1024]{2,1,0:T(8,128)}, s32[]{:T(128)}, s32[384,16,3]{2,0,1:T(8,128)}, s32[]{:T(128)}, /*index=5*/f32[]{:T(128)}, s32[4915...) while((s32[]{:T(128)}, f32[3,128,1024]{2,1,0:T(8,128)}, ...), condition=%wide.region_8.9_spmd.clone, body=%wide.region_6.8_spmd.clone.sunk | while | flops 607670528 | bytes 33094600 | solution.py:124
  475.5 6.7 fusion.92
  482.2 12.3 %scatter_fusion = f32[3,128,1024]{2,1,0:T(8,128)} fusion(f32[3,128,1024]{2,1,0:T(8,128)} %get-tuple-element.1005, s32[9]{0:T(128)S(1)} %reshape.610, f32[9,128,1024]{2,1,0:T(8,128)} %fusion.92), kind=kCustom, calls=%fused_computation.8.clone.clone.1 | custom fusion | flops 1179648 | bytes 14155812 | tf_op jit(solution)/shard_map/while/body/eval_jaxpr/scatter-add | solution.py:115
  509.7 12.2 %scatter_fusion = f32[3,128,1024]{2,1,0:T(8,128)} fusion(f32[3,128,1024]{2,1,0:T(8,128)} %get-tuple-element.1005, s32[9]{0:T(128)S(1)} %reshape.610, f32[9,128,1024]{2,1,0:T(8,128)} %fusion.92), kind=kCustom, calls=%fused_computation.8.clone.clone.1 | custom fusion | flops 1179648 | bytes 14155812 | tf_op jit(solution)/shard_map/while/body/eval_jaxpr/scatter-add | solution.py:115
  536.9 12.5 %scatter_fusion = f32[3,128,1024]{2,1,0:T(8,128)} fusion(f32[3,128,1024]{2,1,0:T(8,128)} %get-tuple-element.1005, s32[9]{0:T(128)S(1)} %reshape.610, f32[9,128,1024]{2,1,0:T(8,128)} %fusion.92), kind=kCustom, calls=%fused_computation.8.clone.clone.1 | custom fusion | flops 1179648 | bytes 14155812 | tf_op jit(solution)/shard_map/while/body/eval_jaxpr/scatter-add | solution.py:115
  564.5 12.4 %scatter_fusion = f32[3,128,1024]{2,1,0:T(8,128)} fusion(f32[3,128,1024]{2,1,0:T(8,128)} %get-tuple-element.1005, s32[9]{0:T(128)S(1)} %reshape.610, f32[9,128,1024]{2,1,0:T(8,128)} %fusion.92), kind=kCustom, calls=%fused_computation.8.clone.clone.1 | custom fusion | flops 1179648 | bytes 14155812 | tf_op jit(solution)/shard_map/while/body/eval_jaxpr/scatter-add | solution.py:115
  592.0 12.5 %scatter_fusion = f32[3,128,1024]{2,1,0:T(8,128)} fusion(f32[3,128,1024]{2,1,0:T(8,128)} %get-tuple-element.1005, s32[9]{0:T(128)S(1)} %reshape.610, f32[9,128,1024]{2,1,0:T(8,128)} %fusion.92), kind=kCustom, calls=%fused_computation.8.clone.clone.1 | custom fusion | flops 1179648 | bytes 14155812 | tf_op jit(solution)/shard_map/while/body/eval_jaxpr/scatter-add | solution.py:115
  612.9 6.7 fusion.92
  619.6 12.0 %scatter_fusion = f32[3,128,1024]{2,1,0:T(8,128)} fusion(f32[3,128,1024]{2,1,0:T(8,128)} %get-tuple-element.1005, s32[9]{0:T(128)S(1)} %reshape.610, f32[9,128,1024]{2,1,0:T(8,128)} %fusion.92), kind=kCustom, calls=%fused_computation.8.clone.clone.1 | custom fusion | flops 1179648 | bytes 14155812 | tf_op jit(solution)/shard_map/while/body/eval_jaxpr/scatter-add | solution.py:115
  646.8 12.3 %scatter_fusion = f32[3,128,1024]{2,1,0:T(8,128)} fusion(f32[3,128,1024]{2,1,0:T(8,128)} %get-tuple-element.1005, s32[9]{0:T(128)S(1)} %reshape.610, f32[9,128,1024]{2,1,0:T(8,128)} %fusion.92), kind=kCustom, calls=%fused_computation.8.clone.clone.1 | custom fusion | flops 1179648 | bytes 14155812 | tf_op jit(solution)/shard_map/while/body/eval_jaxpr/scatter-add | solution.py:115
  667.5 6.7 fusion.92
  674.2 12.2 %scatter_fusion = f32[3,128,1024]{2,1,0:T(8,128)} fusion(f32[3,128,1024]{2,1,0:T(8,128)} %get-tuple-element.1005, s32[9]{0:T(128)S(1)} %reshape.610, f32[9,128,1024]{2,1,0:T(8,128)} %fusion.92), kind=kCustom, calls=%fused_computation.8.clone.clone.1 | custom fusion | flops 1179648 | bytes 14155812 | tf_op jit(solution)/shard_map/while/body/eval_jaxpr/scatter-add | solution.py:115
  694.8 6.7 fusion.92
  701.5 12.2 %scatter_fusion = f32[3,128,1024]{2,1,0:T(8,128)} fusion(f32[3,128,1024]{2,1,0:T(8,128)} %get-tuple-element.1005, s32[9]{0:T(128)S(1)} %reshape.610, f32[9,128,1024]{2,1,0:T(8,128)} %fusion.92), kind=kCustom, calls=%fused_computation.8.clone.clone.1 | custom fusion | flops 1179648 | bytes 14155812 | tf_op jit(solution)/shard_map/while/body/eval_jaxpr/scatter-add | solution.py:115
  728.8 12.3 %scatter_fusion = f32[3,128,1024]{2,1,0:T(8,128)} fusion(f32[3,128,1024]{2,1,0:T(8,128)} %get-tuple-element.1005, s32[9]{0:T(128)S(1)} %reshape.610, f32[9,128,1024]{2,1,0:T(8,128)} %fusion.92), kind=kCustom, calls=%fused_computation.8.clone.clone.1 | custom fusion | flops 1179648 | bytes 14155812 | tf_op jit(solution)/shard_map/while/body/eval_jaxpr/scatter-add | solution.py:115
  756.2 12.5 %scatter_fusion = f32[3,128,1024]{2,1,0:T(8,128)} fusion(f32[3,128,1024]{2,1,0:T(8,128)} %get-tuple-element.1005, s32[9]{0:T(128)S(1)} %reshape.610, f32[9,128,1024]{2,1,0:T(8,128)} %fusion.92), kind=kCustom, calls=%fused_computation.8.clone.clone.1 | custom fusion | flops 1179648 | bytes 14155812 | tf_op jit(solution)/shard_map/while/body/eval_jaxpr/scatter-add | solution.py:115
  777.1 6.7 fusion.92
  783.8 12.3 %scatter_fusion = f32[3,128,1024]{2,1,0:T(8,128)} fusion(f32[3,128,1024]{2,1,0:T(8,128)} %get-tuple-element.1005, s32[9]{0:T(128)S(1)} %reshape.610, f32[9,128,1024]{2,1,0:T(8,128)} %fusion.92), kind=kCustom, calls=%fused_computation.8.clone.clone.1 | custom fusion | flops 1179648 | bytes 14155812 | tf_op jit(solution)/shard_map/while/body/eval_jaxpr/scatter-add | solution.py:115
  804.5 6.7 fusion.92
  811.2 12.5 %scatter_fusion = f32[3,128,1024]{2,1,0:T(8,128)} fusion(f32[3,128,1024]{2,1,0:T(8,128)} %get-tuple-element.1005, s32[9]{0:T(128)S(1)} %reshape.610, f32[9,128,1024]{2,1,0:T(8,128)} %fusion.92), kind=kCustom, calls=%fused_computation.8.clone.clone.1 | custom fusion | flops 1179648 | bytes 14155812 | tf_op jit(solution)/shard_map/while/body/eval_jaxpr/scatter-add | solution.py:115
  838.8 12.3 %scatter_fusion = f32[3,128,1024]{2,1,0:T(8,128)} fusion(f32[3,128,1024]{2,1,0:T(8,128)} %get-tuple-element.1005, s32[9]{0:T(128)S(1)} %reshape.610, f32[9,128,1024]{2,1,0:T(8,128)} %fusion.92), kind=kCustom, calls=%fused_computation.8.clone.clone.1 | custom fusion | flops 1179648 | bytes 14155812 | tf_op jit(solution)/shard_map/while/body/eval_jaxpr/scatter-add | solution.py:115
  859.5 6.7 fusion.92
  866.2 12.3 %scatter_fusion = f32[3,128,1024]{2,1,0:T(8,128)} fusion(f32[3,128,1024]{2,1,0:T(8,128)} %get-tuple-element.1005, s32[9]{0:T(128)S(1)} %reshape.610, f32[9,128,1024]{2,1,0:T(8,128)} %fusion.92), kind=kCustom, calls=%fused_computation.8.clone.clone.1 | custom fusion | flops 1179648 | bytes 14155812 | tf_op jit(solution)/shard_map/while/body/eval_jaxpr/scatter-add | solution.py:115
  887.0 6.7 fusion.92
  893.7 12.2 %scatter_fusion = f32[3,128,1024]{2,1,0:T(8,128)} fusion(f32[3,128,1024]{2,1,0:T(8,128)} %get-tuple-element.1005, s32[9]{0:T(128)S(1)} %reshape.610, f32[9,128,1024]{2,1,0:T(8,128)} %fusion.92), kind=kCustom, calls=%fused_computation.8.clone.clone.1 | custom fusion | flops 1179648 | bytes 14155812 | tf_op jit(solution)/shard_map/while/body/eval_jaxpr/scatter-add | solution.py:115
  (912 shorter events, 541.3 us)
Async XLA Ops:
  7.2 99.7 %all-gather.3.cloned.1.call-start = ((), (), s32[]{:S(2)}) async-start(), calls=%async_computation.2 | async-start | bytes 13369344 | tf_op jit(solution)/shard_map/all_gather | solution.py:127
  10.8 7.0 copy-start.15
  10.8 18.6 %all-to-all-start = ((bf16[8,384,128]{2,1,0:T(8,128)(2,1)}), bf16[8,384,128]{2,1,0:T(8,128)(2,1)S(1)}, u32[]{:S(2)}, u32[]{:S(2)}) async-start(bf16[8,384,128]{2,1,0:T(8,128)(2,1)} %bitcast), calls=%async_computation | async-start | bytes 1572864 | tf_op jit(solution)/shard_map/all_to_all | solution.py:46
  17.7 448.0 %all-gather.5.cloned.1.call-start = ((), (), s32[]{:S(2)}) async-start(), calls=%async_computation.3 | async-start | bytes 13369344 | tf_op jit(solution)/shard_map/all_gather | solution.py:128
  29.4 5.0 copy-start.9
  36.7 70.2 %copy-start.11 = (s32[49152]{0:T(1024)S(1)}, s32[49152]{0:T(1024)}, u32[]{:S(2)}) copy-start(s32[49152]{0:T(1024)} %param.15) | copy-start | bytes 589828
  113.5 2.9 copy-start.5
  123.3 3.1 copy-start.2
  134.8 2.9 copy-start.5
  144.4 4.2 copy-start.2
  156.9 2.9 copy-start.5
  166.4 3.1 copy-start.2
  177.9 2.9 copy-start.5
  187.9 3.1 copy-start.2
  199.4 2.9 copy-start.5
  208.9 3.1 copy-start.2
  220.4 2.9 copy-start.5
  229.9 3.1 copy-start.2
  250.9 3.1 copy-start.2
  271.9 3.1 copy-start.2
  292.9 3.1 copy-start.2
  313.9 3.1 copy-start.2
  334.9 3.1 copy-start.2
  355.8 3.1 copy-start.2
  367.3 2.9 copy-start.5
  376.8 3.1 copy-start.2
  397.8 3.1 copy-start.2
  409.2 2.9 copy-start.5
  418.8 3.1 copy-start.2
  439.8 3.1 copy-start.2
  449.7 17.5 %copy-start.1 = (bf16[384,1024]{1,0:T(8,128)(2,1)S(1)}, bf16[384,1024]{1,0:T(8,128)(2,1)}, u32[]{:S(2)}) copy-start(bf16[384,1024]{1,0:T(8,128)(2,1)} %fusion.57) | copy-start | bytes 2359300
  449.7 16.1 %all-to-all-start.1 = ((bf16[384,8,128]{2,0,1:T(8,128)(2,1)}), bf16[384,8,128]{2,0,1:T(8,128)(2,1)S(1)}, u32[]{:S(2)}, u32[]{:S(2)}) async-start(bf16[384,8,128]{2,0,1:T(8,128)(2,1)} %fusion.68), calls=%async_computation.1 | async-start | bytes 1572864 | tf_op jit(solution)/shard_map/all_to_all | solution.py:130
  (33 other events, 57.9 us)
Sparse Core Ops, SparseCore 0:
  11.0 95.8 all-gather.2
  109.3 88.6 all-gather.4
where the time goes:
time: 925 us; the launch traced here: 917 us
  other arithmetic  317 us (34%)
  local copies, waits for them, and re-layouts  271 us (29%)
  matrix products  214 us (23%)
  waiting for transfers between devices  87.6 us (9%)
  between operations  14.1 us (2%)
  starting transfers between devices  11.4 us (1%)
    scatter-add x16, other arithmetic, image_step(): return image_acc.at[local_tile].add(update)  197 us
    dot_general x16, matrix products, text_step(): jnp.einsum('cij,cjd->cid', weights, remote, preferred_element_type=jnp.fl...  107 us
    dot_general x16, matrix products, image_step(): jnp.einsum('cij,cid->cjd', weights, sender_text, preferred_element_type=j...  107 us
    all_gather x1, waiting for transfers between devices, per_device(): lax.all_gather(image_unit, 'blk', axis=0, tiled=True)  69.1 us
    reduce_sum x16, other arithmetic, text_step(): return text_acc + update.reshape(tile_count, SLOTS, TILE, width).sum(axis=1)  50.7 us
    broadcast_in_dim x16, local copies, waits for them, and re-layouts, per_device(): text_repeat = jnp.repeat(text_tiles, SLOTS, axis=0)  46.3 us
    dynamic_slice x32, local copies, waits for them, and re-layouts, one_shard(): shard = lax.dynamic_slice_in_dim(piece, offset * row_count, row_count, 0)  37.9 us
    gather x16, local copies, waits for them, and re-layouts, image_step(): mine = image_tiles[local_tile]  36.8 us
  transfers between devices with their start and end apart: 4, of which 3 were waited for; matrix products, arithmetic and copies ran while one was open for 36% of the time, Pallas kernels for 0%

commit v1 on v0

v1 whole, which is shorter than its diff:
```python
import jax
import jax.numpy as jnp
from jax import lax
from jax.experimental import pallas as pl
from jax.experimental.pallas import tpu as pltpu
from jax.sharding import PartitionSpec as P

MESH = pl.DeviceIdType.MESH
F32 = jnp.float32
BF16 = jnp.bfloat16
TILE = 128
TILES = 3
SLOTS = 3
ROWS = TILE * TILES
HALF = ROWS // 2
E = 1024
GROUPS = 8
EB = E // GROUPS
LOG2E = 1.4426950408889634
NT = (((1,), (1,)), ((), ()))
NN = (((1,), (0,)), ((), ()))
TN = (((0,), (0,)), ((), ()))


def kernel(
    scale_ref, bias_ref, text_hbm, image_hbm, bucket_hbm, positive_hbm, blocks_hbm,
    tgrad_hbm, igrad_hbm,
    traw, iraw, bucket_v, positive_v, blocks_v,
    T, I, W, rowb, cnt, trs, irs,
    tacc, lacc, iacc, send_t, send_y, send_x, got_c0, got_c1, got_y, got_l, got_r,
    relay_l, relay_r, gbuf, gimg,
    loc_sem, a2a_s, a2a_r, xs, xr, xfs, xfr, cs, cr, ys, yr, fs, fr,
    c0s, c0r, c1s, c1r, y2s, y2r, x2s, x2r, o_s, o_r,
):
    blk = lax.axis_index("blk")
    tp = lax.axis_index("tp")
    yh = blk // 8
    x = (blk // 2) % 4
    c = blk % 2
    core_dev = (blk + 1 - 2 * c, tp)
    yh_blk = (blk + 8) % 16
    y_dev = (yh_blk, tp)
    right = ((yh * 4 + (x + 1) % 4) * 2 + c, tp)
    left = ((yh * 4 + (x + 3) % 4) * 2 + c, tp)
    far_blk = (yh * 4 + (x + 2) % 4) * 2 + c
    image_blk = (blk, left[0], right[0], far_blk)
    text_blk = (blk, core_dev[0], yh_blk, yh_blk + 1 - 2 * c)

    def remote(src, dst, ssem, rsem, dev):
        return pltpu.make_async_remote_copy(
            src_ref=src, dst_ref=dst, send_sem=ssem, recv_sem=rsem,
            device_id=dev, device_id_type=MESH,
        )

    local = [
        pltpu.make_async_copy(image_hbm, iraw, loc_sem.at[0]),
        pltpu.make_async_copy(bucket_hbm, bucket_v, loc_sem.at[1]),
        pltpu.make_async_copy(positive_hbm, positive_v, loc_sem.at[2]),
    ]
    local.append(pltpu.make_async_copy(blocks_hbm, blocks_v, loc_sem.at[3]))
    own_text = pltpu.make_async_copy(
        text_hbm.at[pl.ds(pl.multiple_of(tp * ROWS, ROWS), ROWS)], traw.at[tp], loc_sem.at[7]
    )
    for cp in local:
        cp.start()
    own_text.start()

    barrier = pltpu.get_barrier_semaphore()
    peers = [(blk, (tp + k) % GROUPS) for k in range(1, GROUPS)]
    peers += [core_dev, y_dev, right, left]
    for dev in peers:
        pl.semaphore_signal(barrier, inc=1, device_id=dev, device_id_type=MESH)
    pl.semaphore_wait(barrier, len(peers))

    a2a = []
    for j in range(TILES):
        row = []
        for k in range(1, GROUPS):
            to = (tp + k) % GROUPS
            start = pl.multiple_of(to * ROWS + j * TILE, TILE)
            cp = remote(
                text_hbm.at[pl.ds(start, TILE)],
                traw.at[tp, pl.ds(j * TILE, TILE)],
                a2a_s.at[j, k - 1], a2a_r.at[j, k - 1], (blk, to),
            )
            cp.start()
            row.append(cp)
        a2a.append(row)

    local[0].wait()

    def image_half(h):
        rows = pl.ds(h * HALF, HALF)
        v = iraw[rows, :].astype(F32)
        r = lax.rsqrt(jnp.sum(v * v, axis=-1, keepdims=True) + 1e-6)
        irs[rows, :] = r
        I[rows, :] = (v * r).astype(BF16)

    def image_send(h, side):
        dev = right if side == 0 else left
        return remote(
            I.at[pl.ds(h * HALF, HALF)],
            I.at[pl.ds((1 + side) * ROWS + h * HALF, HALF)],
            xs.at[side, h], xr.at[side, h], dev,
        )

    ring = {(h, s): image_send(h, s) for h in range(2) for s in range(2)}
    image_half(0)
    ring[0, 0].start()
    image_half(1)
    ring[1, 1].start()
    ring[1, 0].start()
    ring[0, 1].start()

    scale = scale_ref[0]
    bias = bias_ref[0]
    ea = -scale * LOG2E
    eb = -bias * LOG2E
    for cp in local[1:]:
        cp.wait()

    def spread(row):
        return jnp.broadcast_to(row.astype(F32), (TILE, TILE)).T

    for s in range(4):
        def prep(j, carry, s=s):
            r = (text_blk[s] * GROUPS + tp) * TILES + j
            block = j + (TILES if s >= 2 else 0)
            rowb[block, pl.ds((s % 2) * TILE, TILE), :] = spread(bucket_v[pl.ds(r, 1), :])
            lanes = lax.broadcasted_iota(jnp.int32, blocks_v.shape[1:], 1)
            for l in range(TILES):
                n = sum(jnp.where(blocks_v[m] == l, 1.0, 0.0) for m in range(SLOTS))
                n = jnp.sum(jnp.where(lanes == r, n, 0.0), axis=1, keepdims=True)
                cnt[2 * block + s % 2, l] = jnp.broadcast_to(n * scale, (blocks_v.shape[1], TILE))
            return carry

        lax.fori_loop(0, TILES, prep, 0)

    own_text.wait()
    to_core, to_y, fwd_y = [], [], []
    for j in range(TILES):
        to_core.append(remote(T.at[j, pl.ds(0, TILE)], T.at[j, pl.ds(TILE, TILE)], cs.at[j], cr.at[j], core_dev))
        to_y.append(remote(T.at[j, pl.ds(0, TILE)], T.at[TILES + j, pl.ds(0, TILE)], ys.at[j], yr.at[j], y_dev))
        fwd_y.append(
            remote(T.at[TILES + j, pl.ds(0, TILE)], T.at[TILES + j, pl.ds(TILE, TILE)], fs.at[j], fr.at[j], core_dev)
        )

    def text_tile(j):
        for cp in a2a[j]:
            cp.wait_recv()
        rows = pl.ds(j * TILE, TILE)
        total = jnp.zeros((TILE, 1), F32)
        sq = jnp.zeros((TILE, EB), F32)
        for g in range(GROUPS):
            v = traw[g, rows, :].astype(F32)
            sq = sq + v * v
        total = jnp.sum(sq, axis=-1, keepdims=True)
        r = lax.rsqrt(total + 1e-6)
        trs[rows, :] = r
        for g in range(GROUPS):
            T[j, 0:TILE, g * EB : (g + 1) * EB] = (traw[g, rows, :].astype(F32) * r).astype(BF16)
        to_core[j].start()
        to_y[j].start()

    text_tile(0)
    text_tile(1)
    on_right = remote(
        I.at[pl.ds(ROWS, HALF)], I.at[pl.ds(3 * ROWS, HALF)], xfs.at[0], xfr.at[0], right
    )
    on_left = remote(
        I.at[pl.ds(2 * ROWS + HALF, HALF)], I.at[pl.ds(3 * ROWS + HALF, HALF)],
        xfs.at[1], xfr.at[1], left,
    )
    ring[0, 0].wait_recv()
    on_right.start()
    ring[1, 1].wait_recv()
    on_left.start()
    text_tile(2)

    def weights(lo, hi, k0, nk):
        cols = pl.ds(k0 * ROWS, nk * ROWS)

        def body(b, carry):
            s = lax.dot_general(T[b], I[cols, :], NT, preferred_element_type=F32)
            d = 1.0 + jnp.exp2(s * ea + eb)
            for h in range(2):
                rb = rowb[b, pl.ds(h * TILE, TILE), :]
                for k in range(nk):
                    shard = image_blk[k0 + k]
                    for l in range(TILES):
                        tile = (shard * GROUPS + tp) * TILES + l
                        cb = bucket_v[pl.ds(tile, 1), :].astype(F32)
                        co = cnt[2 * b + h, l, pl.ds(shard, 1), :]
                        at = (k * TILES + l) * TILE
                        dd = d[h * TILE : (h + 1) * TILE, at : at + TILE]
                        w = jnp.where(rb == cb, co, 0.0) / dd
                        W[b, pl.ds(h * TILE, TILE), pl.ds(k0 * ROWS + at, TILE)] = w.astype(BF16)
            return carry

        lax.fori_loop(lo, hi, body, 0)

    def own_pairs():
        def body(j, carry):
            at = pl.multiple_of(j * TILE, TILE)
            s = lax.dot_general(
                T[j, 0:TILE, :], I[pl.ds(at, TILE), :], NT, preferred_element_type=F32
            )
            e = jnp.exp2(s * ea + eb)
            tile = (blk * GROUPS + tp) * TILES + j
            rb = rowb[j, 0:TILE, :]
            cb = bucket_v[pl.ds(tile, 1), :].astype(F32)
            co = cnt[2 * j, j, pl.ds(blk, 1), :]
            pos = spread(positive_v[pl.ds(tile, 1), :] - tile * TILE)
            matched = pos == lax.broadcasted_iota(jnp.int32, (TILE, TILE), 1).astype(F32)
            num = jnp.where(matched, -co * e, jnp.where(rb == cb, co, 0.0))
            W[j, 0:TILE, pl.ds(at, TILE)] = (num / (1.0 + e)).astype(BF16)
            return carry

        lax.fori_loop(0, TILES, body, 0)

    for cp in to_core:
        cp.wait_recv()
    weights(0, 3, 0, 1)
    own_pairs()
    to_y[0].wait_recv()
    fwd_y[0].start()
    ring[1, 0].wait_recv()
    ring[0, 1].wait_recv()
    weights(0, 3, 1, 2)
    to_y[1].wait_recv()
    fwd_y[1].start()
    fwd_y[0].wait_recv()
    weights(3, 4, 0, 3)
    to_y[2].wait_recv()
    fwd_y[2].start()
    fwd_y[1].wait_recv()
    weights(4, 5, 0, 3)
    fwd_y[2].wait_recv()
    weights(5, 6, 0, 3)
    on_right.wait_recv()
    on_left.wait_recv()
    weights(0, 6, 3, 1)

    c1 = [
        remote(send_t.at[1, pl.ds(j * TILE, TILE)], got_c1.at[pl.ds(j * TILE, TILE)], c1s.at[j], c1r.at[j], core_dev)
        for j in range(TILES)
    ]
    c0 = [
        remote(send_t.at[0, pl.ds(j * TILE, TILE)], got_c0.at[pl.ds(j * TILE, TILE)], c0s.at[j], c0r.at[j], core_dev)
        for j in range(TILES)
    ]
    y2 = [
        remote(send_y.at[pl.ds(j * TILE, TILE)], got_y.at[pl.ds(j * TILE, TILE)], y2s.at[j], y2r.at[j], y_dev)
        for j in range(TILES)
    ]

    def text_sums(b, acc, j, which):
        u = lax.dot_general(W[b], I[...], NN, preferred_element_type=F32)
        acc[pl.ds(j * TILE, TILE), :] = u[0:TILE]
        send_t[which, pl.ds(j * TILE, TILE), :] = u[TILE:].astype(BF16)

    for j in range(TILES):
        text_sums(TILES + j, lacc, j, 1)
        c1[j].start()

    def image_sums(k):
        out = jnp.zeros((ROWS, E), F32)
        for b in range(2 * TILES):
            out = out + lax.dot_general(
                W[b, :, pl.ds(k * ROWS, ROWS)], T[b], TN, preferred_element_type=F32
            )
        return out

    first = pl.ds(0, HALF)
    second = pl.ds(HALF, HALF)
    send_x[2] = image_sums(3).astype(BF16)
    far_right = remote(send_x.at[2, first], relay_l, x2s.at[0], x2r.at[0], right)
    far_left = remote(send_x.at[2, second], relay_r, x2s.at[1], x2r.at[1], left)
    far_right.start()
    far_left.start()

    for j in range(TILES):
        rows = pl.ds(j * TILE, TILE)
        c1[j].wait_recv()
        send_y[rows, :] = (lacc[rows, :] + got_c1[rows, :].astype(F32)).astype(BF16)
        y2[j].start()

    send_x[1] = image_sums(2).astype(BF16)
    near_right = remote(send_x.at[1, second], got_l.at[second], x2s.at[2], x2r.at[2], right)
    near_right.start()
    send_x[0] = image_sums(1).astype(BF16)
    near_left = remote(send_x.at[0, first], got_r.at[first], x2s.at[3], x2r.at[3], left)
    near_left.start()

    for j in range(TILES):
        text_sums(j, tacc, j, 0)
        c0[j].start()
    iacc[...] = image_sums(0)

    far_right.wait_recv()
    send_x[1, first, :] = (send_x[1, first, :].astype(F32) + relay_l[...].astype(F32)).astype(BF16)
    sum_right = remote(send_x.at[1, first], got_l.at[first], x2s.at[4], x2r.at[4], right)
    sum_right.start()
    far_left.wait_recv()
    send_x[0, second, :] = (send_x[0, second, :].astype(F32) + relay_r[...].astype(F32)).astype(BF16)
    sum_left = remote(send_x.at[0, second], got_r.at[second], x2s.at[5], x2r.at[5], left)
    sum_left.start()

    back = []
    for j in range(TILES):
        rows = pl.ds(j * TILE, TILE)
        c0[j].wait_recv()
        y2[j].wait_recv()
        r = trs[rows, :]
        up = tacc[rows, :] + got_c0[rows, :].astype(F32) + got_y[rows, :].astype(F32)
        dot = jnp.zeros((TILE, EB), F32)
        for g in range(GROUPS):
            dot = dot + traw[g, rows, :].astype(F32) * r * up[:, g * EB : (g + 1) * EB]
        d = jnp.sum(dot, axis=-1, keepdims=True)
        for g in range(GROUPS):
            u = traw[g, rows, :].astype(F32) * r
            gbuf[g, rows, :] = (r * (up[:, g * EB : (g + 1) * EB] - u * d)).astype(BF16)
        start = pl.multiple_of(tp * ROWS + j * TILE, TILE)
        for k in range(1, GROUPS):
            to = (tp + k) % GROUPS
            cp = remote(
                gbuf.at[to, rows], tgrad_hbm.at[pl.ds(start, TILE)],
                o_s.at[j, k - 1], o_r.at[j, k - 1], (blk, to),
            )
            cp.start()
            back.append(cp)
    own_out = pltpu.make_async_copy(
        gbuf.at[tp], tgrad_hbm.at[pl.ds(pl.multiple_of(tp * ROWS, ROWS), ROWS)], loc_sem.at[8]
    )
    own_out.start()

    near_right.wait_recv()
    near_left.wait_recv()
    sum_right.wait_recv()
    sum_left.wait_recv()
    v = iraw[...].astype(F32) * irs[...]
    up = iacc[...] + got_l[...].astype(F32) + got_r[...].astype(F32)
    d = jnp.sum(v * up, axis=-1, keepdims=True)
    gimg[...] = (irs[...] * (up - v * d)).astype(BF16)
    image_out = pltpu.make_async_copy(gimg, igrad_hbm, loc_sem.at[9])
    image_out.start()

    for row in a2a:
        for cp in row:
            cp.wait_send()
    for cp in ring.values():
        cp.wait_send()
    sent = [on_right, on_left, far_right, far_left, near_right, near_left, sum_right, sum_left]
    for cp in sent + to_core + to_y + fwd_y + c0 + c1 + y2:
        cp.wait_send()
    for cp in back:
        cp.wait()
    own_out.wait()
    image_out.wait()


def per_device(text_emb, image_emb, logit_scale, logit_bias, bucket, positive, blocks):
    any_spec = pl.BlockSpec(memory_space=pl.ANY)
    smem_spec = pl.BlockSpec(memory_space=pltpu.SMEM)
    vm = pltpu.VMEM
    dma = pltpu.SemaphoreType.DMA
    tiles = bucket.shape[0] // TILE
    return pl.pallas_call(
        kernel,
        out_shape=(
            jax.ShapeDtypeStruct(text_emb.shape, BF16),
            jax.ShapeDtypeStruct(image_emb.shape, BF16),
        ),
        in_specs=[smem_spec, smem_spec] + [any_spec] * 5,
        out_specs=(any_spec, any_spec),
        scratch_shapes=[
            vm((GROUPS, ROWS, EB), BF16), vm((ROWS, E), BF16),
            vm((tiles, TILE), jnp.int32), vm((tiles, TILE), jnp.int32), vm(blocks.shape[::-1], jnp.int32),
            vm((6, 256, E), BF16), vm((4 * ROWS, E), BF16), vm((6, 256, 4 * ROWS), BF16),
            vm((6, 256, TILE), F32), vm((12, TILES, 16, TILE), F32),
            vm((ROWS, 1), F32), vm((ROWS, 1), F32),
            vm((ROWS, E), F32), vm((ROWS, E), F32), vm((ROWS, E), F32),
            vm((2, ROWS, E), BF16), vm((ROWS, E), BF16), vm((3, ROWS, E), BF16),
            vm((ROWS, E), BF16), vm((ROWS, E), BF16), vm((ROWS, E), BF16),
            vm((ROWS, E), BF16), vm((ROWS, E), BF16),
            vm((HALF, E), BF16), vm((HALF, E), BF16),
            vm((GROUPS, ROWS, EB), BF16), vm((ROWS, E), BF16),
            dma((10,)), dma((3, 7)), dma((3, 7)),
            dma((2, 2)), dma((2, 2)), dma((2,)), dma((2,)),
            dma((3,)), dma((3,)), dma((3,)), dma((3,)), dma((3,)), dma((3,)),
            dma((3,)), dma((3,)), dma((3,)), dma((3,)), dma((3,)), dma((3,)),
            dma((6,)), dma((6,)), dma((3, 7)), dma((3, 7)),
        ],
        compiler_params=pltpu.CompilerParams(
            collective_id=0, has_side_effects=True, vmem_limit_bytes=56 << 20
        ),
        name="pairs",
    )(
        logit_scale, logit_bias, text_emb, image_emb,
        bucket.reshape(tiles, TILE), positive.reshape(tiles, TILE), blocks.transpose(2, 1, 0),
    )


def solution(mesh):
    in_specs = (P("blk", "tp"), P(("blk", "tp"), None), P(), P(), P(), P(), P())
    out_specs = (P("blk", "tp"), P(("blk", "tp"), None))
    return jax.shard_map(
        per_device, mesh=mesh, in_specs=in_specs, out_specs=out_specs, check_vma=False
    )
```

time: 925 us -> 81.9 us (0.09)
  other arithmetic: 317 us -> 0 us
  local copies, waits for them, and re-layouts: 271 us -> 3.02 us
  matrix products: 214 us -> 0 us
  waiting for transfers between devices: 87.6 us -> 0 us
  Pallas kernels: 0 us -> 76.8 us
  between operations: 14.1 us -> 1.94 us
  starting transfers between devices: 11.4 us -> 0 us
    dot_general x32 -> x0, matrix products: 214 us -> none  [the longest x16 107 us: text_step(): jnp.einsum('cij,cjd->cid', weights, remote, preferred_element_type=jnp.fl...]
    scatter-add x16 -> x0, other arithmetic: 197 us -> none  [image_step(): return image_acc.at[local_tile].add(update)]
    gather x113 -> x0, local copies, waits for them, and re-layouts: 109 us -> none  [the longest x16 36.8 us: image_step(): mine = image_tiles[local_tile]]
    pallas_call x0 -> x1, Pallas kernels: none -> 76.8 us  [per_device(): pl.pallas_call(kernel, out_shape=(jax.ShapeDtypeStruct(text_emb.shape, BF...]
    all_gather x2 -> x0, waiting for transfers between devices: 69.1 us -> none  [the longest x1 69.1 us: per_device(): lax.all_gather(image_unit, 'blk', axis=0, tiled=True)]
    broadcast_in_dim x66 -> x0, local copies, waits for them, and re-layouts: 54.8 us -> none  [the longest x16 46.3 us: per_device(): text_repeat = jnp.repeat(text_tiles, SLOTS, axis=0)]
    reduce_sum x20 -> x0, other arithmetic: 54.7 us -> none  [the longest x16 50.7 us: text_step(): return text_acc + update.reshape(tile_count, SLOTS, TILE, width).sum(axis=1)]
    dynamic_slice x33 -> x0, local copies, waits for them, and re-layouts: 38.8 us -> none  [the longest x32 37.9 us: one_shard(): shard = lax.dynamic_slice_in_dim(piece, offset * row_count, row_count, 0)]
  transfers between devices with their start and end apart: 4 -> 0, of which waited for: 3 -> 0; matrix products, arithmetic and copies ran while one was open for 36% -> 0% of each run, Pallas kernels for 0% -> 0%
where the time goes in v1:
time: 81.9 us; the launch traced here: 81.7 us
  Pallas kernels  76.8 us (94%)
  local copies, waits for them, and re-layouts  3.02 us (4%)
  between operations  1.94 us (2%)
    pallas_call x1, Pallas kernels, per_device(): pl.pallas_call(kernel, out_shape=(jax.ShapeDtypeStruct(text_emb.shape, BF...  76.8 us
    unnamed x4, local copies, waits for them, and re-layouts  3.02 us

profile of v1, /device:TPU:1, one launch (start us, length us, event | category | flops | bytes accessed | tf_op | source)
XLA Modules:
  0.0 81.7 jit_solution(1425182171539197316)
XLA Ops:
  1.9 76.8 %pairs.1 = (bf16[3072,128]{1,0:T(8,128)(2,1)}, bf16[384,1024]{1,0:T(8,128)(2,1)}) custom-call(f32[1]{0:T(128)S(6)} %copy.11.scale_ref, f32[1]{0:T(128)S(6)} %copy.12.bias_ref, bf16[3072,128]{1,0:T(8,128)(2,1)} %text_hbm.1, bf16[384,1024]{1,0:T(8,128)(2,1)} %image_hbm.1, s32[384,128]{1,0:T(8,128)} %bitcast.3, s32[384,128]{1,0:T(8,128)} %bitcast.4, ...), custom_call_target="tpu_custom_call" | custom-call | tf_op jit(solution)/shard_map/pairs/pallas_call | solution.py:368
  78.7 0.0 copy-start
  78.7 2.1 %copy.13 = bf16[3072,128]{1,0:T(8,128)(2,1)} copy(bf16[3072,128]{1,0:T(8,128)(2,1)} %get-tuple-element.4) | data formatting | bytes 1572864
  80.9 0.0 copy-done
  80.9 0.9 %copy.14 = bf16[384,1024]{1,0:T(8,128)(2,1)} copy(bf16[384,1024]{1,0:T(8,128)(2,1)S(1)} %copy-done) | data formatting | bytes 1572864
Async XLA Ops:
  78.7 2.1 %copy-start = (bf16[384,1024]{1,0:T(8,128)(2,1)S(1)}, bf16[384,1024]{1,0:T(8,128)(2,1)}, u32[]{:S(2)}) copy-start(bf16[384,1024]{1,0:T(8,128)(2,1)} %get-tuple-element.5) | copy-start | bytes 2359300

commit v2 on v1

v2 whole, which is shorter than its diff:
```python
import jax
import jax.numpy as jnp
from jax import lax
from jax.experimental import pallas as pl
from jax.experimental.pallas import tpu as pltpu
from jax.sharding import PartitionSpec as P

MESH = pl.DeviceIdType.MESH
F32 = jnp.float32
BF16 = jnp.bfloat16
TILE = 128
TILES = 3
SLOTS = 3
ROWS = TILE * TILES
HALF = ROWS // 2
PARTS = 3
E = 1024
GROUPS = 8
EB = E // GROUPS
LOG2E = 1.4426950408889634
NT = (((1,), (1,)), ((), ()))
NN = (((1,), (0,)), ((), ()))
TN = (((0,), (0,)), ((), ()))


def kernel(
    scale_ref, bias_ref, text_hbm, image_hbm, bucket_hbm, positive_hbm, blocks_hbm,
    tgrad_out, igrad_out,
    R, pas, iraw, bucket_v, positive_v, blocks_v,
    T, I, W, rowb, cnt, trs, irs,
    tacc, iacc, pacc, send_t, send_x, got_c, got_l, got_r, relay_l, relay_r,
    keep, gsend, got_far, got_pair, got_other, gout,
    loc_sem, zs, zr, xs, xr, xfs, xfr, ys, yr, cs, cr, ps, pr, gs, gr, x2s, x2r, o_s, o_r,
):
    blk = lax.axis_index("blk")
    tp = lax.axis_index("tp")
    yh = blk // 8
    x = (blk // 2) % 4
    c = blk % 2
    z = tp // 2
    yl = tp % 2
    yh_blk = (blk + 8) % 16
    tp_pair = tp + 1 - 2 * yl
    core_dev = (blk + 1 - 2 * c, tp)
    far_y = (yh_blk, tp)
    pair_y = (blk, tp_pair)
    other_y = (yh_blk, tp_pair)
    z_devs = [(k, (blk, ((z + k) % 4) * 2 + yl)) for k in range(1, 4)]
    right = ((yh * 4 + (x + 1) % 4) * 2 + c, tp)
    left = ((yh * 4 + (x + 3) % 4) * 2 + c, tp)
    far_blk = (yh * 4 + (x + 2) % 4) * 2 + c
    image_blk = (blk, left[0], right[0], far_blk)
    text_blk = ((blk, core_dev[0]), (yh_blk, yh_blk + 1 - 2 * c))

    def remote(src, dst, ssem, rsem, dev):
        return pltpu.make_async_remote_copy(
            src_ref=src, dst_ref=dst, send_sem=ssem, recv_sem=rsem,
            device_id=dev, device_id_type=MESH,
        )

    def drain(ref, sem):
        pltpu.make_async_copy(ref, ref, sem).wait()

    local = [
        pltpu.make_async_copy(image_hbm, iraw, loc_sem.at[0]),
        pltpu.make_async_copy(bucket_hbm, bucket_v, loc_sem.at[1]),
        pltpu.make_async_copy(positive_hbm, positive_v, loc_sem.at[2]),
        pltpu.make_async_copy(blocks_hbm, blocks_v, loc_sem.at[3]),
    ]
    def own_rows(d):
        return pl.ds(pl.multiple_of((z * 2 + d) * ROWS, ROWS), ROWS)

    own_text = [
        pltpu.make_async_copy(text_hbm.at[own_rows(yl)], R.at[0, yl, z], loc_sem.at[6]),
        pltpu.make_async_copy(text_hbm.at[own_rows(1 - yl)], pas.at[z], loc_sem.at[7]),
    ]
    for cp in local:
        cp.start()
    for cp in own_text:
        cp.start()

    barrier = pltpu.get_barrier_semaphore()
    peers = [dev for _, dev in z_devs] + [far_y, pair_y, other_y, core_dev, right, left]
    for dev in peers:
        pl.semaphore_signal(barrier, inc=1, device_id=dev, device_id_type=MESH)

    local[0].wait()
    for h in range(2):
        rows = pl.ds(h * HALF, HALF)
        v = iraw[rows, :].astype(F32)
        r = lax.rsqrt(jnp.sum(v * v, axis=-1, keepdims=True) + 1e-6)
        irs[rows, :] = r
        I[rows, :] = (v * r).astype(BF16)

    pl.semaphore_wait(barrier, len(peers))

    def z_send(j):
        rows = pl.ds(j * TILE, TILE)
        for k, dev in z_devs:
            base = ((z + k) % 4) * 2
            for same in range(2):
                d = 1 - yl if same == 0 else yl
                start = pl.multiple_of((base + d) * ROWS + j * TILE, TILE)
                dst = R.at[0, yl, z, rows] if same else pas.at[z, rows]
                remote(text_hbm.at[pl.ds(start, TILE)], dst, zs, zr.at[j, same], dev).start()

    z_send(0)

    def image_send(h, side):
        return remote(
            I.at[pl.ds(h * HALF, HALF)],
            I.at[pl.ds((1 + side) * ROWS + h * HALF, HALF)],
            xs, xr.at[side, h], right if side == 0 else left,
        )

    ring = {(h, s): image_send(h, s) for h in range(2) for s in range(2)}
    ring[0, 0].start()
    ring[1, 1].start()

    for cp in local[1:]:
        cp.wait()
    scale = scale_ref[0]
    bias = bias_ref[0]
    ea = -scale * LOG2E
    eb = -bias * LOG2E

    def spread(row):
        return jnp.broadcast_to(row.astype(F32), (TILE, TILE)).T

    for side in range(2):
        for core in range(2):
            def prep(j, carry, side=side, core=core):
                r = (text_blk[side][core] * GROUPS + tp) * TILES + j
                block = 2 * j + side
                rowb[block, pl.ds(core * TILE, TILE), :] = spread(bucket_v[pl.ds(r, 1), :])
                lanes = lax.broadcasted_iota(jnp.int32, blocks_v.shape[1:], 1)
                for l in range(TILES):
                    n = sum(jnp.where(blocks_v[m] == l, 1.0, 0.0) for m in range(SLOTS))
                    n = jnp.sum(jnp.where(lanes == r, n, 0.0), axis=1, keepdims=True)
                    cnt[2 * block + core, l] = jnp.broadcast_to(n * scale, (blocks_v.shape[1], TILE))
                return carry

            lax.fori_loop(0, TILES, prep, 0)

    z_send(1)

    for cp in own_text:
        cp.wait()
    along_y, to_core = [], []
    for j in range(TILES):
        rows = pl.ds(j * TILE, TILE)
        along_y.append([
            remote(pas.at[:, rows], R.at[0, yl, :, rows], ys.at[j], yr.at[j, 0], pair_y),
            remote(pas.at[:, rows], R.at[1, yl, :, rows], ys.at[j], yr.at[j, 1], other_y),
            remote(R.at[0, yl, :, rows], R.at[1, yl, :, rows], ys.at[j], yr.at[j, 2], far_y),
        ])
        to_core.append([
            remote(T.at[2 * j + side, pl.ds(0, TILE)], T.at[2 * j + side, pl.ds(TILE, TILE)], cs, cr.at[j, side], core_dev)
            for side in range(2)
        ])

    def z_ready(j):
        rows = pl.ds(j * TILE, TILE)
        drain(pas.at[pl.ds(0, 3), rows], zr.at[j, 0])
        drain(R.at[0, 0, pl.ds(0, 3), rows], zr.at[j, 1])

    def pass_on(j):
        for cp in along_y[j]:
            cp.start()

    def text_tile(j, side):
        rows = pl.ds(j * TILE, TILE)
        if side == 0:
            along_y[j][0].wait_recv()
        else:
            along_y[j][1].wait_recv()
            along_y[j][2].wait_recv()
        sq = jnp.zeros((TILE, EB), F32)
        for d in range(2):
            for g in range(4):
                v = R[side, d, g, rows, :].astype(F32)
                sq = sq + v * v
        r = lax.rsqrt(jnp.sum(sq, axis=-1, keepdims=True) + 1e-6)
        trs[side, rows, :] = r
        for d in range(2):
            for g in range(4):
                at = (2 * g + d) * EB
                T[2 * j + side, 0:TILE, at : at + EB] = (R[side, d, g, rows, :].astype(F32) * r).astype(BF16)
        to_core[j][side].start()

    def text_ready(j):
        for cp in to_core[j]:
            cp.wait_recv()

    z_ready(0)
    pass_on(0)
    z_send(2)
    z_ready(1)
    ring[1, 0].start()
    ring[0, 1].start()
    drain(pas, ys.at[0])
    pass_on(1)
    on_right = remote(
        I.at[pl.ds(ROWS, HALF)], I.at[pl.ds(3 * ROWS, HALF)], xfs, xfr.at[0], right
    )
    on_left = remote(
        I.at[pl.ds(2 * ROWS + HALF, HALF)], I.at[pl.ds(3 * ROWS + HALF, HALF)],
        xfs, xfr.at[1], left,
    )

    def weights(lo, hi, k0, nk):
        cols = pl.ds(k0 * ROWS, nk * ROWS)

        def body(b, carry):
            s = lax.dot_general(T[b], I[cols, :], NT, preferred_element_type=F32)
            d = 1.0 + jnp.exp2(s * ea + eb)
            for h in range(2):
                rb = rowb[b, pl.ds(h * TILE, TILE), :]
                for k in range(nk):
                    shard = image_blk[k0 + k]
                    for l in range(TILES):
                        tile = (shard * GROUPS + tp) * TILES + l
                        cb = bucket_v[pl.ds(tile, 1), :].astype(F32)
                        co = cnt[2 * b + h, l, pl.ds(shard, 1), :]
                        at = (k * TILES + l) * TILE
                        dd = d[h * TILE : (h + 1) * TILE, at : at + TILE]
                        w = jnp.where(rb == cb, co, 0.0) / dd
                        W[b, pl.ds(h * TILE, TILE), pl.ds(k0 * ROWS + at, TILE)] = w.astype(BF16)
            return carry

        lax.fori_loop(lo, hi, body, 0)

    def own_pairs():
        def body(j, carry):
            at = pl.multiple_of(j * TILE, TILE)
            s = lax.dot_general(
                T[2 * j, 0:TILE, :], I[pl.ds(at, TILE), :], NT, preferred_element_type=F32
            )
            e = jnp.exp2(s * ea + eb)
            tile = (blk * GROUPS + tp) * TILES + j
            rb = rowb[2 * j, 0:TILE, :]
            cb = bucket_v[pl.ds(tile, 1), :].astype(F32)
            co = cnt[4 * j, j, pl.ds(blk, 1), :]
            pos = spread(positive_v[pl.ds(tile, 1), :] - tile * TILE)
            matched = pos == lax.broadcasted_iota(jnp.int32, (TILE, TILE), 1).astype(F32)
            num = jnp.where(matched, -co * e, jnp.where(rb == cb, co, 0.0))
            W[2 * j, 0:TILE, pl.ds(at, TILE)] = (num / (1.0 + e)).astype(BF16)
            return carry

        lax.fori_loop(0, TILES, body, 0)

    def image_sums(k, lo, hi):
        out = None
        for b in range(lo, hi):
            u = lax.dot_general(
                W[b, :, pl.ds(k * ROWS, ROWS)], T[b], TN, preferred_element_type=F32
            )
            out = u if out is None else out + u
        return out

    text_tile(0, 0)
    text_tile(0, 1)
    z_ready(2)
    text_ready(0)
    weights(0, 2, 0, 1)
    drain(pas, ys.at[1])
    pass_on(2)
    ring[0, 0].wait_recv()
    on_right.start()
    ring[1, 1].wait_recv()
    on_left.start()
    text_tile(1, 0)
    text_tile(1, 1)
    text_ready(1)
    ring[1, 0].wait_recv()
    ring[0, 1].wait_recv()
    weights(0, 4, 1, 2)
    pacc[0] = image_sums(2, 0, 4)
    pacc[1] = image_sums(1, 0, 4)
    text_tile(2, 0)
    text_tile(2, 1)
    weights(2, 4, 0, 1)
    text_ready(2)
    weights(4, 6, 1, 2)
    first = pl.ds(0, HALF)
    second = pl.ds(HALF, HALF)
    send_x[1] = (pacc[0] + image_sums(2, 4, 6)).astype(BF16)
    near_right = remote(send_x.at[1, second], got_l.at[second], x2s, x2r.at[0], right)
    near_right.start()
    send_x[0] = (pacc[1] + image_sums(1, 4, 6)).astype(BF16)
    near_left = remote(send_x.at[0, first], got_r.at[first], x2s, x2r.at[1], left)
    near_left.start()

    weights(4, 6, 0, 1)
    own_pairs()
    on_right.wait_recv()
    on_left.wait_recv()
    weights(0, 6, 3, 1)
    partial = [
        remote(send_t.at[b], got_c.at[b], ps, pr.at[b], core_dev) for b in range(2 * TILES)
    ]

    def text_sums(b):
        u = lax.dot_general(W[b], I[...], NN, preferred_element_type=F32)
        tacc[b] = u[0:TILE]
        send_t[b] = u[TILE:].astype(BF16)
        partial[b].start()

    back = []
    for j in range(TILES):
        rows = pl.ds(j * TILE, TILE)
        back.append([
            remote(gsend.at[0, 1 - yl, :, rows], got_pair.at[:, rows], gs, gr.at[j, 0], pair_y),
            remote(gsend.at[1, 1 - yl, :, rows], got_other.at[:, rows], gs, gr.at[j, 1], other_y),
            remote(gsend.at[1, yl, :, rows], got_far.at[:, rows], gs, gr.at[j, 2], far_y),
        ])

    def project(j, side):
        b = 2 * j + side
        rows = pl.ds(j * TILE, TILE)
        partial[b].wait_recv()
        r = trs[side, rows, :]
        up = tacc[b] + got_c[b].astype(F32)
        dot = jnp.zeros((TILE, EB), F32)
        for d in range(2):
            for g in range(4):
                at = (2 * g + d) * EB
                dot = dot + R[side, d, g, rows, :].astype(F32) * r * up[:, at : at + EB]
        total = jnp.sum(dot, axis=-1, keepdims=True)
        for d in range(2):
            for g in range(4):
                at = (2 * g + d) * EB
                u = R[side, d, g, rows, :].astype(F32) * r
                out = r * (up[:, at : at + EB] - u * total)
                gsend[side, d, g, rows, :] = out.astype(BF16)
                if side == 0:
                    keep[d, g, rows, :] = out
        if side == 0:
            back[j][0].start()
        else:
            back[j][1].start()
            back[j][2].start()

    def feature_rows(j):
        rows = pl.ds(j * TILE, TILE)
        for cp in back[j]:
            cp.wait_recv()
        for g in range(4):
            gout[0, g, rows, :] = (
                got_pair[g, rows, :].astype(F32) + got_other[g, rows, :].astype(F32)
            ).astype(BF16)
            gout[1, g, rows, :] = (keep[yl, g, rows, :] + got_far[g, rows, :].astype(F32)).astype(BF16)
        for same in range(2):
            d = 1 - yl if same == 0 else yl
            start = pl.multiple_of((z * 2 + d) * ROWS + j * TILE, TILE)
            for k, dev in z_devs:
                remote(gout.at[same, (z + k) % 4, rows], tgrad_out.at[pl.ds(start, TILE)], o_s, o_r, dev).start()

    PART = HALF // PARTS
    far, summed = {}, {}
    for n in range(PARTS):
        for side, (relay, got, dev) in enumerate(((relay_l, got_l, right), (relay_r, got_r, left))):
            rows = pl.ds(side * HALF + n * PART, PART)
            far[n, side] = remote(
                send_x.at[2, rows], relay.at[pl.ds(n * PART, PART)], x2s, x2r.at[2 + 2 * n + side], dev
            )
            summed[n, side] = remote(
                send_x.at[1 - side, rows], got.at[rows], x2s, x2r.at[2 + 2 * (PARTS + n) + side], dev
            )

    def send_far():
        send_x[2] = image_sums(3, 0, 6).astype(BF16)
        for cp in far.values():
            cp.start()

    def combine(n):
        for side, relay in enumerate((relay_l, relay_r)):
            rows = pl.ds(side * HALF + n * PART, PART)
            far[n, side].wait_recv()
            send_x[1 - side, rows, :] = (
                send_x[1 - side, rows, :].astype(F32) + relay[pl.ds(n * PART, PART), :].astype(F32)
            ).astype(BF16)
            summed[n, side].start()

    text_sums(1)
    text_sums(0)
    project(0, 1)
    text_sums(3)
    project(0, 0)
    send_far()
    text_sums(2)
    project(1, 1)
    text_sums(5)
    project(1, 0)
    text_sums(4)
    project(2, 1)
    iacc[...] = image_sums(0, 0, 6)
    project(2, 0)
    combine(0)
    feature_rows(0)
    combine(1)
    combine(2)
    feature_rows(1)
    feature_rows(2)
    own_out = [
        pltpu.make_async_copy(
            gout.at[same, z], tgrad_out.at[own_rows(1 - yl if same == 0 else yl)], loc_sem.at[8 + same]
        )
        for same in range(2)
    ]
    for cp in own_out:
        cp.start()

    near_right.wait_recv()
    near_left.wait_recv()
    for cp in summed.values():
        cp.wait_recv()
    v = iraw[...].astype(F32) * irs[...]
    up = iacc[...] + got_l[...].astype(F32) + got_r[...].astype(F32)
    d = jnp.sum(v * up, axis=-1, keepdims=True)
    igrad_out[...] = (irs[...] * (up - v * d)).astype(BF16)

    drain(text_hbm.at[pl.ds(0, 6 * ROWS)], zs)
    drain(pas, ys.at[2])
    drain(R.at[:, :, pl.ds(0, 3)], gs)
    drain(I.at[pl.ds(0, 2 * ROWS)], cs)
    drain(I.at[pl.ds(0, 2 * ROWS)], ps)
    drain(I.at[pl.ds(0, ROWS)], xfs)
    drain(I.at[pl.ds(0, 2 * ROWS)], xs)
    drain(I.at[pl.ds(0, 3 * ROWS)], x2s)
    drain(text_hbm.at[pl.ds(0, 6 * ROWS)], o_s)
    drain(tgrad_out.at[pl.ds(0, 6 * ROWS)], o_r)
    for cp in own_out:
        cp.wait()


def per_device(text_emb, image_emb, logit_scale, logit_bias, bucket, positive, blocks):
    vmem_spec = pl.BlockSpec(memory_space=pltpu.VMEM)
    hbm_spec = pl.BlockSpec(memory_space=pltpu.HBM)
    vm = pltpu.VMEM
    dma = pltpu.SemaphoreType.DMA
    tiles = bucket.shape[0] // TILE
    shapes = (
        pltpu.VMEM(text_emb.shape, BF16),
        pltpu.VMEM(image_emb.shape, BF16),
    )
    return pl.pallas_call(
        kernel,
        out_shape=shapes,
        in_specs=[pl.BlockSpec(memory_space=pltpu.SMEM)] * 2 + [hbm_spec] * 5,
        out_specs=(vmem_spec, vmem_spec),
        scratch_shapes=[
            vm((2, 2, 4, ROWS, EB), BF16), vm((4, ROWS, EB), BF16), vm((ROWS, E), BF16),
            vm((tiles, TILE), jnp.int32), vm((tiles, TILE), jnp.int32), vm(blocks.shape[::-1], jnp.int32),
            vm((6, 256, E), BF16), vm((4 * ROWS, E), BF16), vm((6, 256, 4 * ROWS), BF16),
            vm((6, 256, TILE), F32), vm((12, TILES, 16, TILE), F32),
            vm((2, ROWS, 1), F32), vm((ROWS, 1), F32),
            vm((6, TILE, E), F32), vm((ROWS, E), F32), vm((2, ROWS, E), F32),
            vm((6, TILE, E), BF16), vm((3, ROWS, E), BF16), vm((6, TILE, E), BF16),
            vm((ROWS, E), BF16), vm((ROWS, E), BF16), vm((HALF, E), BF16), vm((HALF, E), BF16),
            vm((2, 4, ROWS, EB), F32), vm((2, 2, 4, ROWS, EB), BF16),
            vm((4, ROWS, EB), BF16), vm((4, ROWS, EB), BF16), vm((4, ROWS, EB), BF16),
            vm((2, 4, ROWS, EB), BF16),
            dma((10,)), dma, dma((3, 2)), dma, dma((2, 2)), dma, dma((2,)),
            dma((3,)), dma((3, 3)), dma, dma((3, 2)), dma, dma((6,)), dma, dma((3, 3)),
            dma, dma((2 + 4 * PARTS,)), dma, dma,
        ],
        compiler_params=pltpu.CompilerParams(
            collective_id=0, has_side_effects=True, vmem_limit_bytes=48 << 20
        ),
        name="pairs",
    )(
        logit_scale, logit_bias,
        *(
            pltpu.with_memory_space_constraint(a, pltpu.HBM)
            for a in (
                text_emb, image_emb,
                bucket.reshape(tiles, TILE), positive.reshape(tiles, TILE), blocks.transpose(2, 1, 0),
            )
        )
    )


def solution(mesh):
    in_specs = (P("blk", "tp"), P(("blk", "tp"), None), P(), P(), P(), P(), P())
    out_specs = (P("blk", "tp"), P(("blk", "tp"), None))
    return jax.shard_map(
        per_device, mesh=mesh, in_specs=in_specs, out_specs=out_specs, check_vma=False
    )
```

time: 81.9 us -> 72.4 us (0.88)
  Pallas kernels: 76.8 us -> 68.6 us
  local copies, waits for them, and re-layouts: 3.02 us -> 1.76 us
    pallas_call x1, Pallas kernels: 76.8 us -> 68.6 us  [per_device(): pl.pallas_call(kernel, out_shape=shapes, in_specs=[pl.BlockSpec(memory_sp...]
    unnamed x4 -> x2, local copies, waits for them, and re-layouts: 3.02 us -> 1.76 us
where the time goes in v2:
time: 72.4 us; the launch traced here: 72.3 us
  Pallas kernels  68.6 us (95%)
  between operations  1.93 us (3%)
  local copies, waits for them, and re-layouts  1.76 us (2%)
    pallas_call x1, Pallas kernels, per_device(): pl.pallas_call(kernel, out_shape=shapes, in_specs=[pl.BlockSpec(memory_sp...  68.6 us
    unnamed x2, local copies, waits for them, and re-layouts  1.76 us

profile of v2, /device:TPU:1, one launch (start us, length us, event | category | flops | bytes accessed | tf_op | source)
XLA Modules:
  0.0 72.3 jit_solution(14530397593300261770)
XLA Ops:
  1.9 68.6 %pairs.1 = (bf16[3072,128]{1,0:T(8,128)(2,1)S(1)}, bf16[384,1024]{1,0:T(8,128)(2,1)S(1)}) custom-call(f32[1]{0:T(128)S(6)} %copy.13.scale_ref, f32[1]{0:T(128)S(6)} %copy.14.bias_ref, bf16[3072,128]{1,0:T(8,128)(2,1)} %text_hbm.1, bf16[384,1024]{1,0:T(8,128)(2,1)} %image_hbm.1, s32[384,128]{1,0:T(8,128)} %bitcast.3, s32[384,128]{1,0:T(8,128)} %bitcast.4, ...), custom_call_target="tpu_custom_call" | custom-call | tf_op jit(solution)/shard_map/pairs/pallas_call | solution.py:447
  70.5 0.9 %copy.11 = bf16[3072,128]{1,0:T(8,128)(2,1)} copy(bf16[3072,128]{1,0:T(8,128)(2,1)S(1)} %get-tuple-element.2) | data formatting | bytes 1572864
  71.4 0.9 %copy.12 = bf16[384,1024]{1,0:T(8,128)(2,1)} copy(bf16[384,1024]{1,0:T(8,128)(2,1)S(1)} %get-tuple-element.3) | data formatting | bytes 1572864

commit v3 on v2

--- a/solution.py
+++ b/solution.py
@@ -13,6 +13,7 @@
 SLOTS = 3
 ROWS = TILE * TILES
 HALF = ROWS // 2
+CHUNKS = 4
 PARTS = 3
 E = 1024
 GROUPS = 8
@@ -27,10 +28,10 @@
     scale_ref, bias_ref, text_hbm, image_hbm, bucket_hbm, positive_hbm, blocks_hbm,
     tgrad_out, igrad_out,
     R, pas, iraw, bucket_v, positive_v, blocks_v,
-    T, I, W, rowb, cnt, trs, irs,
-    tacc, iacc, pacc, send_t, send_x, got_c, got_l, got_r, relay_l, relay_r,
+    T, I, W, M, rowb, cnt, trs, irs,
+    tacc, iacc, send_t, send_x, got_c, got_l, got_r, relay_l, relay_r,
     keep, gsend, got_far, got_pair, got_other, gout,
-    loc_sem, zs, zr, xs, xr, xfs, xfr, ys, yr, cs, cr, ps, pr, gs, gr, x2s, x2r, o_s, o_r,
+    loc_sem, zs, zr, xs, xr, xfs, xfr, y0s, y0r, ys, yr, cs, cr, ps, pr, gs, gr, x2s, x2r, o_s, o_r,
 ):
     blk = lax.axis_index("blk")
     tp = lax.axis_index("tp")
@@ -70,14 +71,10 @@
     def own_rows(d):
         return pl.ds(pl.multiple_of((z * 2 + d) * ROWS, ROWS), ROWS)
 
-    own_text = [
-        pltpu.make_async_copy(text_hbm.at[own_rows(yl)], R.at[0, yl, z], loc_sem.at[6]),
-        pltpu.make_async_copy(text_hbm.at[own_rows(1 - yl)], pas.at[z], loc_sem.at[7]),
-    ]
+    own_text = pltpu.make_async_copy(text_hbm.at[own_rows(yl)], R.at[0, yl, z], loc_sem.at[6])
     for cp in local:
         cp.start()
-    for cp in own_text:
-        cp.start()
+    own_text.start()
 
     barrier = pltpu.get_barrier_semaphore()
     peers = [dev for _, dev in z_devs] + [far_y, pair_y, other_y, core_dev, right, left]
@@ -105,6 +102,13 @@
                 remote(text_hbm.at[pl.ds(start, TILE)], dst, zs, zr.at[j, same], dev).start()
 
     z_send(0)
+    held = [
+        remote(text_hbm.at[own_rows(1 - yl)], R.at[0, yl, z], y0s, y0r.at[0], pair_y),
+        remote(text_hbm.at[own_rows(1 - yl)], R.at[1, yl, z], y0s, y0r.at[1], other_y),
+        remote(text_hbm.at[own_rows(yl)], R.at[1, yl, z], y0s, y0r.at[2], far_y),
+    ]
+    for cp in held:
+        cp.start()
 
     def image_send(h, side):
         return remote(
@@ -137,25 +141,42 @@
                 for l in range(TILES):
                     n = sum(jnp.where(blocks_v[m] == l, 1.0, 0.0) for m in range(SLOTS))
                     n = jnp.sum(jnp.where(lanes == r, n, 0.0), axis=1, keepdims=True)
-                    cnt[2 * block + core, l] = jnp.broadcast_to(n * scale, (blocks_v.shape[1], TILE))
+                    cnt[2 * block + core, l] = jnp.broadcast_to(n, (blocks_v.shape[1], TILE))
                 return carry
 
             lax.fori_loop(0, TILES, prep, 0)
 
     z_send(1)
 
-    for cp in own_text:
-        cp.wait()
+    def pair_masks(b, carry):
+        for k in range(4):
+            for l in range(TILES):
+                cb = bucket_v[pl.ds((image_blk[k] * GROUPS + tp) * TILES + l, 1), :].astype(F32)
+                for h in range(2):
+                    rows = pl.ds(pl.multiple_of((2 * b + h) * TILE, TILE), TILE)
+                    n = cnt[2 * b + h, l, pl.ds(image_blk[k], 1), :]
+                    M[rows, pl.ds(k * ROWS + l * TILE, TILE)] = jnp.where(
+                        rowb[b, pl.ds(h * TILE, TILE), :] == cb, n, 0.0
+                    ).astype(BF16)
+        return carry
+
+    lax.fori_loop(0, 2 * TILES, pair_masks, 0)
+
+    own_text.wait()
     along_y, to_core = [], []
     for j in range(TILES):
         rows = pl.ds(j * TILE, TILE)
-        along_y.append([
-            remote(pas.at[:, rows], R.at[0, yl, :, rows], ys.at[j], yr.at[j, 0], pair_y),
-            remote(pas.at[:, rows], R.at[1, yl, :, rows], ys.at[j], yr.at[j, 1], other_y),
-            remote(R.at[0, yl, :, rows], R.at[1, yl, :, rows], ys.at[j], yr.at[j, 2], far_y),
-        ])
+        pieces = []
+        for k in range(1, 4):
+            zk = (z + k) % 4
+            pieces += [
+                remote(pas.at[zk, rows], R.at[0, yl, zk, rows], ys.at[j], yr.at[j, 0], pair_y),
+                remote(pas.at[zk, rows], R.at[1, yl, zk, rows], ys.at[j], yr.at[j, 1], other_y),
+                remote(R.at[0, yl, zk, rows], R.at[1, yl, zk, rows], ys.at[j], yr.at[j, 2], far_y),
+            ]
+        along_y.append(pieces)
         to_core.append([
-            remote(T.at[2 * j + side, pl.ds(0, TILE)], T.at[2 * j + side, pl.ds(TILE, TILE)], cs, cr.at[j, side], core_dev)
+            remote(T.at[pl.ds((4 * j + 2 * side) * TILE, TILE)], T.at[pl.ds((4 * j + 2 * side + 1) * TILE, TILE)], cs, cr.at[j, side], core_dev)
             for side in range(2)
         ])
 
@@ -170,11 +191,10 @@
 
     def text_tile(j, side):
         rows = pl.ds(j * TILE, TILE)
-        if side == 0:
-            along_y[j][0].wait_recv()
-        else:
-            along_y[j][1].wait_recv()
-            along_y[j][2].wait_recv()
+        for kind in (0,) if side == 0 else (1, 2):
+            if j == 0:
+                held[kind].wait_recv()
+            drain(pas.at[pl.ds(0, 3), rows], yr.at[j, kind])
         sq = jnp.zeros((TILE, EB), F32)
         for d in range(2):
             for g in range(4):
@@ -185,7 +205,7 @@
         for d in range(2):
             for g in range(4):
                 at = (2 * g + d) * EB
-                T[2 * j + side, 0:TILE, at : at + EB] = (R[side, d, g, rows, :].astype(F32) * r).astype(BF16)
+                T[pl.ds((4 * j + 2 * side) * TILE, TILE), at : at + EB] = (R[side, d, g, rows, :].astype(F32) * r).astype(BF16)
         to_core[j][side].start()
 
     def text_ready(j):
@@ -196,10 +216,11 @@
     pass_on(0)
     z_send(2)
     z_ready(1)
+    pass_on(1)
     ring[1, 0].start()
     ring[0, 1].start()
-    drain(pas, ys.at[0])
-    pass_on(1)
+    z_ready(2)
+    pass_on(2)
     on_right = remote(
         I.at[pl.ds(ROWS, HALF)], I.at[pl.ds(3 * ROWS, HALF)], xfs, xfr.at[0], right
     )
@@ -211,60 +232,31 @@
     def weights(lo, hi, k0, nk):
         cols = pl.ds(k0 * ROWS, nk * ROWS)
 
-        def body(b, carry):
-            s = lax.dot_general(T[b], I[cols, :], NT, preferred_element_type=F32)
-            d = 1.0 + jnp.exp2(s * ea + eb)
-            for h in range(2):
-                rb = rowb[b, pl.ds(h * TILE, TILE), :]
-                for k in range(nk):
-                    shard = image_blk[k0 + k]
-                    for l in range(TILES):
-                        tile = (shard * GROUPS + tp) * TILES + l
-                        cb = bucket_v[pl.ds(tile, 1), :].astype(F32)
-                        co = cnt[2 * b + h, l, pl.ds(shard, 1), :]
-                        at = (k * TILES + l) * TILE
-                        dd = d[h * TILE : (h + 1) * TILE, at : at + TILE]
-                        w = jnp.where(rb == cb, co, 0.0) / dd
-                        W[b, pl.ds(h * TILE, TILE), pl.ds(k0 * ROWS + at, TILE)] = w.astype(BF16)
-            return carry
-
-        lax.fori_loop(lo, hi, body, 0)
-
-    def own_pairs():
-        def body(j, carry):
-            at = pl.multiple_of(j * TILE, TILE)
-            s = lax.dot_general(
-                T[2 * j, 0:TILE, :], I[pl.ds(at, TILE), :], NT, preferred_element_type=F32
-            )
-            e = jnp.exp2(s * ea + eb)
-            tile = (blk * GROUPS + tp) * TILES + j
-            rb = rowb[2 * j, 0:TILE, :]
-            cb = bucket_v[pl.ds(tile, 1), :].astype(F32)
-            co = cnt[4 * j, j, pl.ds(blk, 1), :]
-            pos = spread(positive_v[pl.ds(tile, 1), :] - tile * TILE)
-            matched = pos == lax.broadcasted_iota(jnp.int32, (TILE, TILE), 1).astype(F32)
-            num = jnp.where(matched, -co * e, jnp.where(rb == cb, co, 0.0))
-            W[2 * j, 0:TILE, pl.ds(at, TILE)] = (num / (1.0 + e)).astype(BF16)
-            return carry
-
-        lax.fori_loop(0, TILES, body, 0)
-
-    def image_sums(k, lo, hi):
-        out = None
         for b in range(lo, hi):
-            u = lax.dot_general(
-                W[b, :, pl.ds(k * ROWS, ROWS)], T[b], TN, preferred_element_type=F32
-            )
-            out = u if out is None else out + u
-        return out
+            rows = pl.ds(b * 2 * TILE, 2 * TILE)
+            s = lax.dot_general(T[rows, :], I[cols, :], NT, preferred_element_type=F32)
+            w = pl.reciprocal(1.0 + jnp.exp2(s * ea + eb)).astype(BF16)
+            W[rows, cols] = w * M[rows, cols]
+
+    def own_pairs(j):
+        at = j * TILE
+        s = lax.dot_general(T[4 * at : 4 * at + TILE, :], I[at : at + TILE, :], NT, preferred_element_type=F32)
+        e = jnp.exp2(s * ea + eb)
+        tile = (blk * GROUPS + tp) * TILES + j
+        n = cnt[4 * j, j, pl.ds(blk, 1), :]
+        pos = spread(positive_v[pl.ds(tile, 1), :] - tile * TILE)
+        matched = pos == lax.broadcasted_iota(jnp.int32, (TILE, TILE), 1).astype(F32)
+        num = jnp.where(matched, -n * e, M[4 * at : 4 * at + TILE, at : at + TILE].astype(F32))
+        W[4 * at : 4 * at + TILE, at : at + TILE] = (num / (1.0 + e)).astype(BF16)
+
+    def image_sums(k):
+        return lax.dot_general(W[:, pl.ds(k * ROWS, ROWS)], T[...], TN, preferred_element_type=F32)
 
     text_tile(0, 0)
     text_tile(0, 1)
-    z_ready(2)
     text_ready(0)
     weights(0, 2, 0, 1)
-    drain(pas, ys.at[1])
-    pass_on(2)
+    own_pairs(0)
     ring[0, 0].wait_recv()
     on_right.start()
     ring[1, 1].wait_recv()
@@ -272,27 +264,24 @@
     text_tile(1, 0)
     text_tile(1, 1)
     text_ready(1)
+    weights(2, 4, 0, 1)
+    own_pairs(1)
+    text_tile(2, 0)
+    text_tile(2, 1)
+    text_ready(2)
+    weights(4, 6, 0, 1)
+    own_pairs(2)
     ring[1, 0].wait_recv()
     ring[0, 1].wait_recv()
-    weights(0, 4, 1, 2)
-    pacc[0] = image_sums(2, 0, 4)
-    pacc[1] = image_sums(1, 0, 4)
-    text_tile(2, 0)
-    text_tile(2, 1)
-    weights(2, 4, 0, 1)
-    text_ready(2)
-    weights(4, 6, 1, 2)
+    weights(0, 6, 1, 2)
     first = pl.ds(0, HALF)
     second = pl.ds(HALF, HALF)
-    send_x[1] = (pacc[0] + image_sums(2, 4, 6)).astype(BF16)
+    send_x[1] = image_sums(2).astype(BF16)
     near_right = remote(send_x.at[1, second], got_l.at[second], x2s, x2r.at[0], right)
     near_right.start()
-    send_x[0] = (pacc[1] + image_sums(1, 4, 6)).astype(BF16)
+    send_x[0] = image_sums(1).astype(BF16)
     near_left = remote(send_x.at[0, first], got_r.at[first], x2s, x2r.at[1], left)
     near_left.start()
-
-    weights(4, 6, 0, 1)
-    own_pairs()
     on_right.wait_recv()
     on_left.wait_recv()
     weights(0, 6, 3, 1)
@@ -301,7 +290,7 @@
     ]
 
     def text_sums(b):
-        u = lax.dot_general(W[b], I[...], NN, preferred_element_type=F32)
+        u = lax.dot_general(W[pl.ds(b * 2 * TILE, 2 * TILE), :], I[...], NN, preferred_element_type=F32)
         tacc[b] = u[0:TILE]
         send_t[b] = u[TILE:].astype(BF16)
         partial[b].start()
@@ -320,6 +309,7 @@
         rows = pl.ds(j * TILE, TILE)
         partial[b].wait_recv()
         r = trs[side, rows, :]
+        rs = r * scale
         up = tacc[b] + got_c[b].astype(F32)
         dot = jnp.zeros((TILE, EB), F32)
         for d in range(2):
@@ -331,7 +321,7 @@
             for g in range(4):
                 at = (2 * g + d) * EB
                 u = R[side, d, g, rows, :].astype(F32) * r
-                out = r * (up[:, at : at + EB] - u * total)
+                out = rs * (up[:, at : at + EB] - u * total)
                 gsend[side, d, g, rows, :] = out.astype(BF16)
                 if side == 0:
                     keep[d, g, rows, :] = out
@@ -369,7 +359,7 @@
             )
 
     def send_far():
-        send_x[2] = image_sums(3, 0, 6).astype(BF16)
+        send_x[2] = image_sums(3).astype(BF16)
         for cp in far.values():
             cp.start()
 
@@ -394,7 +384,7 @@
     project(1, 0)
     text_sums(4)
     project(2, 1)
-    iacc[...] = image_sums(0, 0, 6)
+    iacc[...] = image_sums(0)
     project(2, 0)
     combine(0)
     feature_rows(0)
@@ -418,10 +408,12 @@
     v = iraw[...].astype(F32) * irs[...]
     up = iacc[...] + got_l[...].astype(F32) + got_r[...].astype(F32)
     d = jnp.sum(v * up, axis=-1, keepdims=True)
-    igrad_out[...] = (irs[...] * (up - v * d)).astype(BF16)
+    igrad_out[...] = (irs[...] * scale * (up - v * d)).astype(BF16)
 
     drain(text_hbm.at[pl.ds(0, 6 * ROWS)], zs)
-    drain(pas, ys.at[2])
+    for j in range(TILES):
+        drain(R.at[0, 0, pl.ds(0, 3)], ys.at[j])
+    drain(R.at[0, 0, pl.ds(0, 3)], y0s)
     drain(R.at[:, :, pl.ds(0, 3)], gs)
     drain(I.at[pl.ds(0, 2 * ROWS)], cs)
     drain(I.at[pl.ds(0, 2 * ROWS)], ps)
@@ -434,6 +426,19 @@
         cp.wait()
 
 
+def write_out(a_ref, b_ref, a_out, b_out, sem):
+    copies = []
+    for src, dst in ((a_ref, a_out), (b_ref, b_out)):
+        step = src.shape[0] // CHUNKS
+        for n in range(CHUNKS):
+            rows = pl.ds(n * step, step)
+            copies.append(pltpu.make_async_copy(src.at[rows], dst.at[rows], sem.at[len(copies)]))
+    for cp in copies:
+        cp.start()
+    for cp in copies:
+        cp.wait()
+
+
 def per_device(text_emb, image_emb, logit_scale, logit_bias, bucket, positive, blocks):
     vmem_spec = pl.BlockSpec(memory_space=pltpu.VMEM)
     hbm_spec = pl.BlockSpec(memory_space=pltpu.HBM)
@@ -444,7 +449,7 @@
         pltpu.VMEM(text_emb.shape, BF16),
         pltpu.VMEM(image_emb.shape, BF16),
     )
-    return pl.pallas_call(
+    grads = pl.pallas_call(
         kernel,
         out_shape=shapes,
         in_specs=[pl.BlockSpec(memory_space=pltpu.SMEM)] * 2 + [hbm_spec] * 5,
@@ -452,17 +457,17 @@
         scratch_shapes=[
             vm((2, 2, 4, ROWS, EB), BF16), vm((4, ROWS, EB), BF16), vm((ROWS, E), BF16),
             vm((tiles, TILE), jnp.int32), vm((tiles, TILE), jnp.int32), vm(blocks.shape[::-1], jnp.int32),
-            vm((6, 256, E), BF16), vm((4 * ROWS, E), BF16), vm((6, 256, 4 * ROWS), BF16),
+            vm((4 * ROWS, E), BF16), vm((4 * ROWS, E), BF16), vm((4 * ROWS, 4 * ROWS), BF16), vm((4 * ROWS, 4 * ROWS), BF16),
             vm((6, 256, TILE), F32), vm((12, TILES, 16, TILE), F32),
             vm((2, ROWS, 1), F32), vm((ROWS, 1), F32),
-            vm((6, TILE, E), F32), vm((ROWS, E), F32), vm((2, ROWS, E), F32),
+            vm((6, TILE, E), F32), vm((ROWS, E), F32),
             vm((6, TILE, E), BF16), vm((3, ROWS, E), BF16), vm((6, TILE, E), BF16),
             vm((ROWS, E), BF16), vm((ROWS, E), BF16), vm((HALF, E), BF16), vm((HALF, E), BF16),
             vm((2, 4, ROWS, EB), F32), vm((2, 2, 4, ROWS, EB), BF16),
             vm((4, ROWS, EB), BF16), vm((4, ROWS, EB), BF16), vm((4, ROWS, EB), BF16),
             vm((2, 4, ROWS, EB), BF16),
             dma((10,)), dma, dma((3, 2)), dma, dma((2, 2)), dma, dma((2,)),
-            dma((3,)), dma((3, 3)), dma, dma((3, 2)), dma, dma((6,)), dma, dma((3, 3)),
+            dma, dma((3,)), dma((3,)), dma((3, 3)), dma, dma((3, 2)), dma, dma((6,)), dma, dma((3, 3)),
             dma, dma((2 + 4 * PARTS,)), dma, dma,
         ],
         compiler_params=pltpu.CompilerParams(
@@ -479,6 +484,17 @@
             )
         )
     )
+    return pl.pallas_call(
+        write_out,
+        out_shape=(
+            jax.ShapeDtypeStruct(text_emb.shape, BF16),
+            jax.ShapeDtypeStruct(image_emb.shape, BF16),
+        ),
+        in_specs=[vmem_spec, vmem_spec],
+        out_specs=(hbm_spec, hbm_spec),
+        scratch_shapes=[dma((2 * CHUNKS,))],
+        name="write_out",
+    )(*(pltpu.with_memory_space_constraint(a, pltpu.VMEM) for a in grads))
 
 
 def solution(mesh):

time: 72.4 us -> 68.2 us (0.942)
  Pallas kernels: 68.6 us -> 66 us
  local copies, waits for them, and re-layouts: 1.76 us -> 0 us
    pallas_call x1, Pallas kernels: 68.6 us -> 64.8 us  [per_device(): pl.pallas_call(kernel, out_shape=shapes, in_specs=[pl.BlockSpec(memory_sp...]
    unnamed x2 -> x0, local copies, waits for them, and re-layouts: 1.76 us -> none
    pallas_call x0 -> x1, Pallas kernels: none -> 1.2 us  [per_device(): pl.pallas_call(write_out, out_shape=(jax.ShapeDtypeStruct(text_emb.shape,...]
where the time goes in v3:
time: 68.2 us; the launch traced here: 68.1 us
  Pallas kernels  66 us (97%)
  between operations  2.09 us (3%)
    pallas_call x1, Pallas kernels, per_device(): pl.pallas_call(kernel, out_shape=shapes, in_specs=[pl.BlockSpec(memory_sp...  64.8 us

profile of v3, /device:TPU:1, one launch (start us, length us, event | category | flops | bytes accessed | tf_op | source)
XLA Modules:
  0.0 68.1 jit_solution(16252881266961475196)
XLA Ops:
  1.9 64.8 %pairs.1 = (bf16[3072,128]{1,0:T(8,128)(2,1)S(1)}, bf16[384,1024]{1,0:T(8,128)(2,1)S(1)}) custom-call(f32[1]{0:T(128)S(6)} %copy.9.scale_ref, f32[1]{0:T(128)S(6)} %copy.10.bias_ref, bf16[3072,128]{1,0:T(8,128)(2,1)} %text_hbm.1, bf16[384,1024]{1,0:T(8,128)(2,1)} %image_hbm.1, s32[384,128]{1,0:T(8,128)} %bitcast.3, s32[384,128]{1,0:T(8,128)} %bitcast.4, ...), custom_call_target="tpu_custom_call" | custom-call | tf_op jit(solution)/shard_map/pairs/pallas_call | solution.py:452
  66.7 1.2 %write_out.1 = (bf16[3072,128]{1,0:T(8,128)(2,1)}, bf16[384,1024]{1,0:T(8,128)(2,1)}) custom-call(bf16[3072,128]{1,0:T(8,128)(2,1)S(1)} %get-tuple-element.4.a_ref, bf16[384,1024]{1,0:T(8,128)(2,1)S(1)} %get-tuple-element.5.b_ref), custom_call_target="tpu_custom_call" | custom-call | tf_op jit(solution)/shard_map/write_out/pallas_call | solution.py:487

commit v4 on v3

--- a/solution.py
+++ b/solution.py
@@ -229,10 +229,10 @@
         xfs, xfr.at[1], left,
     )
 
-    def weights(lo, hi, k0, nk):
+    def weights(blocks, k0, nk):
         cols = pl.ds(k0 * ROWS, nk * ROWS)
 
-        for b in range(lo, hi):
+        for b in blocks:
             rows = pl.ds(b * 2 * TILE, 2 * TILE)
             s = lax.dot_general(T[rows, :], I[cols, :], NT, preferred_element_type=F32)
             w = pl.reciprocal(1.0 + jnp.exp2(s * ea + eb)).astype(BF16)
@@ -255,7 +255,7 @@
     text_tile(0, 0)
     text_tile(0, 1)
     text_ready(0)
-    weights(0, 2, 0, 1)
+    weights((0, 1), 0, 1)
     own_pairs(0)
     ring[0, 0].wait_recv()
     on_right.start()
@@ -264,27 +264,24 @@
     text_tile(1, 0)
     text_tile(1, 1)
     text_ready(1)
-    weights(2, 4, 0, 1)
-    own_pairs(1)
     text_tile(2, 0)
     text_tile(2, 1)
-    text_ready(2)
-    weights(4, 6, 0, 1)
-    own_pairs(2)
     ring[1, 0].wait_recv()
     ring[0, 1].wait_recv()
-    weights(0, 6, 1, 2)
+    weights(range(4), 1, 2)
+    text_ready(2)
+    weights((4, 5), 2, 1)
     first = pl.ds(0, HALF)
     second = pl.ds(HALF, HALF)
     send_x[1] = image_sums(2).astype(BF16)
     near_right = remote(send_x.at[1, second], got_l.at[second], x2s, x2r.at[0], right)
     near_right.start()
+    weights((4, 5), 1, 1)
     send_x[0] = image_sums(1).astype(BF16)
     near_left = remote(send_x.at[0, first], got_r.at[first], x2s, x2r.at[1], left)
     near_left.start()
     on_right.wait_recv()
     on_left.wait_recv()
-    weights(0, 6, 3, 1)
     partial = [
         remote(send_t.at[b], got_c.at[b], ps, pr.at[b], core_dev) for b in range(2 * TILES)
     ]
@@ -331,20 +328,20 @@
             back[j][1].start()
             back[j][2].start()
 
-    def feature_rows(j):
-        rows = pl.ds(j * TILE, TILE)
-        for cp in back[j]:
+    def feature_rows(j, same):
+        rows = pl.ds(j * TILE, TILE)
+        for cp in back[j][2:] if same else back[j][:2]:
             cp.wait_recv()
         for g in range(4):
-            gout[0, g, rows, :] = (
-                got_pair[g, rows, :].astype(F32) + got_other[g, rows, :].astype(F32)
-            ).astype(BF16)
-            gout[1, g, rows, :] = (keep[yl, g, rows, :] + got_far[g, rows, :].astype(F32)).astype(BF16)
-        for same in range(2):
-            d = 1 - yl if same == 0 else yl
-            start = pl.multiple_of((z * 2 + d) * ROWS + j * TILE, TILE)
-            for k, dev in z_devs:
-                remote(gout.at[same, (z + k) % 4, rows], tgrad_out.at[pl.ds(start, TILE)], o_s, o_r, dev).start()
+            if same:
+                out = keep[yl, g, rows, :] + got_far[g, rows, :].astype(F32)
+            else:
+                out = got_pair[g, rows, :].astype(F32) + got_other[g, rows, :].astype(F32)
+            gout[same, g, rows, :] = out.astype(BF16)
+        d = yl if same else 1 - yl
+        start = pl.multiple_of((z * 2 + d) * ROWS + j * TILE, TILE)
+        for k, dev in z_devs:
+            remote(gout.at[same, (z + k) % 4, rows], tgrad_out.at[pl.ds(start, TILE)], o_s, o_r, dev).start()
 
     PART = HALF // PARTS
     far, summed = {}, {}
@@ -372,26 +369,36 @@
             ).astype(BF16)
             summed[n, side].start()
 
+    weights((1,), 3, 1)
     text_sums(1)
+    weights((2, 3), 0, 1)
+    weights((3,), 3, 1)
+    text_sums(3)
+    project(0, 1)
+    weights((0, 2, 4, 5), 3, 1)
     text_sums(0)
-    project(0, 1)
-    text_sums(3)
+    project(1, 1)
+    send_far()
     project(0, 0)
-    send_far()
+    weights((4, 5), 0, 1)
+    text_sums(5)
+    own_pairs(1)
     text_sums(2)
-    project(1, 1)
-    text_sums(5)
+    project(2, 1)
+    combine(0)
+    feature_rows(0, 1)
+    feature_rows(0, 0)
+    own_pairs(2)
+    text_sums(4)
     project(1, 0)
-    text_sums(4)
-    project(2, 1)
+    combine(1)
+    project(2, 0)
+    feature_rows(1, 1)
     iacc[...] = image_sums(0)
-    project(2, 0)
-    combine(0)
-    feature_rows(0)
-    combine(1)
     combine(2)
-    feature_rows(1)
-    feature_rows(2)
+    feature_rows(1, 0)
+    feature_rows(2, 1)
+    feature_rows(2, 0)
     own_out = [
         pltpu.make_async_copy(
             gout.at[same, z], tgrad_out.at[own_rows(1 - yl if same == 0 else yl)], loc_sem.at[8 + same]
@@ -403,12 +410,15 @@
 
     near_right.wait_recv()
     near_left.wait_recv()
-    for cp in summed.values():
-        cp.wait_recv()
-    v = iraw[...].astype(F32) * irs[...]
-    up = iacc[...] + got_l[...].astype(F32) + got_r[...].astype(F32)
-    d = jnp.sum(v * up, axis=-1, keepdims=True)
-    igrad_out[...] = (irs[...] * scale * (up - v * d)).astype(BF16)
+    for n in range(PARTS):
+        for side in range(2):
+            rows = pl.ds(side * HALF + n * PART, PART)
+            summed[n, side].wait_recv()
+            r = irs[rows, :]
+            v = iraw[rows, :].astype(F32) * r
+            up = iacc[rows, :] + got_l[rows, :].astype(F32) + got_r[rows, :].astype(F32)
+            d = jnp.sum(v * up, axis=-1, keepdims=True)
+            igrad_out[rows, :] = (r * scale * (up - v * d)).astype(BF16)
 
     drain(text_hbm.at[pl.ds(0, 6 * ROWS)], zs)
     for j in range(TILES):

time: 68.2 us -> 65.3 us (0.957)
  Pallas kernels: 66 us -> 63.1 us
    pallas_call x1, Pallas kernels: 64.8 us -> 61.9 us  [per_device(): pl.pallas_call(kernel, out_shape=shapes, in_specs=[pl.BlockSpec(memory_sp...]
where the time goes in v4:
time: 65.3 us; the launch traced here: 65.2 us
  Pallas kernels  63.1 us (97%)
  between operations  2.09 us (3%)
    pallas_call x1, Pallas kernels, per_device(): pl.pallas_call(kernel, out_shape=shapes, in_specs=[pl.BlockSpec(memory_sp...  61.9 us

profile of v4, /device:TPU:1, one launch (start us, length us, event | category | flops | bytes accessed | tf_op | source)
XLA Modules:
  0.0 65.2 jit_solution(8136086334017066127)
XLA Ops:
  1.9 61.9 %pairs.1 = (bf16[3072,128]{1,0:T(8,128)(2,1)S(1)}, bf16[384,1024]{1,0:T(8,128)(2,1)S(1)}) custom-call(f32[1]{0:T(128)S(6)} %copy.9.scale_ref, f32[1]{0:T(128)S(6)} %copy.10.bias_ref, bf16[3072,128]{1,0:T(8,128)(2,1)} %text_hbm.1, bf16[384,1024]{1,0:T(8,128)(2,1)} %image_hbm.1, s32[384,128]{1,0:T(8,128)} %bitcast.3, s32[384,128]{1,0:T(8,128)} %bitcast.4, ...), custom_call_target="tpu_custom_call" | custom-call | tf_op jit(solution)/shard_map/pairs/pallas_call | solution.py:462
  63.8 1.2 %write_out.1 = (bf16[3072,128]{1,0:T(8,128)(2,1)}, bf16[384,1024]{1,0:T(8,128)(2,1)}) custom-call(bf16[3072,128]{1,0:T(8,128)(2,1)S(1)} %get-tuple-element.4.a_ref, bf16[384,1024]{1,0:T(8,128)(2,1)S(1)} %get-tuple-element.5.b_ref), custom_call_target="tpu_custom_call" | custom-call | tf_op jit(solution)/shard_map/write_out/pallas_call | solution.py:497

commit v5 on v4

--- a/solution.py
+++ b/solution.py
@@ -81,14 +81,6 @@
     for dev in peers:
         pl.semaphore_signal(barrier, inc=1, device_id=dev, device_id_type=MESH)
 
-    local[0].wait()
-    for h in range(2):
-        rows = pl.ds(h * HALF, HALF)
-        v = iraw[rows, :].astype(F32)
-        r = lax.rsqrt(jnp.sum(v * v, axis=-1, keepdims=True) + 1e-6)
-        irs[rows, :] = r
-        I[rows, :] = (v * r).astype(BF16)
-
     pl.semaphore_wait(barrier, len(peers))
 
     def z_send(j):
@@ -109,6 +101,14 @@
     ]
     for cp in held:
         cp.start()
+
+    local[0].wait()
+    for h in range(2):
+        rows = pl.ds(h * HALF, HALF)
+        v = iraw[rows, :].astype(F32)
+        r = lax.rsqrt(jnp.sum(v * v, axis=-1, keepdims=True) + 1e-6)
+        irs[rows, :] = r
+        I[rows, :] = (v * r).astype(BF16)
 
     def image_send(h, side):
         return remote(

time: 65.3 us -> 65.7 us (level)
  no operation moved by 1% of the time
where the time goes in v5:
time: 65.7 us; the launch traced here: 65.4 us
  Pallas kernels  63.4 us (96%)
  between operations  2.09 us (3%)
    pallas_call x1, Pallas kernels, per_device(): pl.pallas_call(kernel, out_shape=shapes, in_specs=[pl.BlockSpec(memory_sp...  62.2 us

profile of v5, /device:TPU:1, one launch (start us, length us, event | category | flops | bytes accessed | tf_op | source)
XLA Modules:
  0.0 65.4 jit_solution(3471242729023512029)
XLA Ops:
  1.9 62.2 %pairs.1 = (bf16[3072,128]{1,0:T(8,128)(2,1)S(1)}, bf16[384,1024]{1,0:T(8,128)(2,1)S(1)}) custom-call(f32[1]{0:T(128)S(6)} %copy.9.scale_ref, f32[1]{0:T(128)S(6)} %copy.10.bias_ref, bf16[3072,128]{1,0:T(8,128)(2,1)} %text_hbm.1, bf16[384,1024]{1,0:T(8,128)(2,1)} %image_hbm.1, s32[384,128]{1,0:T(8,128)} %bitcast.3, s32[384,128]{1,0:T(8,128)} %bitcast.4, ...), custom_call_target="tpu_custom_call" | custom-call | tf_op jit(solution)/shard_map/pairs/pallas_call | solution.py:462
  64.1 1.2 %write_out.1 = (bf16[3072,128]{1,0:T(8,128)(2,1)}, bf16[384,1024]{1,0:T(8,128)(2,1)}) custom-call(bf16[3072,128]{1,0:T(8,128)(2,1)S(1)} %get-tuple-element.4.a_ref, bf16[384,1024]{1,0:T(8,128)(2,1)S(1)} %get-tuple-element.5.b_ref), custom_call_target="tpu_custom_call" | custom-call | tf_op jit(solution)/shard_map/write_out/pallas_call | solution.py:497
